TPU v7x, 256 devices: a whole 4x4x8 slice. The times are simulated.
256 devices in a mesh: chan: 16 (over z_hi, y, core), tm: 16 (over z_lo, x).
Axes of the slice: x: 4, y: 4, z: 8 (z_hi: 2, z_lo: 4; z = z_hi * 4 + z_lo), core: 2. Of those that a mesh axis runs over, the one named last changes fastest.
Arguments:
- signal: bfloat16 [256, 64, 8192], P('chan', None, 'tm'), may hold values from -6 to 6
- depth_weight: float32 [64, 7], replicated, may hold values from -2 to 2
- point_weight: bfloat16 [64, 64], replicated, may hold values from -0.75 to 0.75
- conv_weight: bfloat16 [3, 3, 64, 64], replicated, may hold values from -0.25 to 0.25
- grad_out: bfloat16 [128, 64, 4096], P('chan', None, 'tm'), may hold values from -6 to 6
Outputs:
- features_out: bfloat16 [128, 64, 4096], P('chan', None, 'tm')
- grad_signal: bfloat16 [256, 64, 8192], P('chan', None, 'tm')
- grad_depth: float32 [64, 7], replicated
- grad_point: float32 [64, 64], replicated
- grad_conv: float32 [3, 3, 64, 64], replicated
All inputs are finite; a program needn't handle non-finite values.
Results may differ from a plain program's by a relative error of at most 0.0065.
Values may be sent and summed in bfloat16 or wider, within the bound.
A program may use at most 64 MiB of HBM per device.

v0:
```python
import jax
import jax.numpy as jnp
from jax import lax
from jax.sharding import PartitionSpec as P

KERNEL_TAPS = 7
DILATION_STEP = 8
RIM = 24


def extended(shard, sides, width):
    for axis, dim in sides:
        size, length = (lax.axis_size(axis), shard.shape[dim])
        up = [(i, (i + 1) % size) for i in range(size - 1)]
        down = [(j, i) for i, j in up]
        last = lax.slice_in_dim(shard, length - width, length, axis=dim)
        first = lax.slice_in_dim(shard, 0, width, axis=dim)
        before = lax.ppermute(last, axis, up)
        after = lax.ppermute(first, axis, down)
        shard = jnp.concatenate([before, shard, after], axis=dim)
    return shard


def passed_along(block, axis, distance):
    devices = range(lax.axis_size(axis))
    route = [(i - distance, i) for i in devices if i - distance in devices]
    return lax.ppermute(block, axis, route)


def depthwise(extended_signal, weight, window_length):
    summed = jnp.zeros(extended_signal.shape[:2] + (window_length,), jnp.float32)
    for kernel_tap_index in range(KERNEL_TAPS):
        tap_segment = extended_signal[
            :,
            :,
            kernel_tap_index * DILATION_STEP : kernel_tap_index * DILATION_STEP + window_length,
        ].astype(jnp.float32)
        summed = summed + weight[:, kernel_tap_index][None, :, None] * tap_segment
    return summed


def conv_down(padded, weight):
    half_rows = (padded.shape[0] - 1) // 2
    half_cols = (padded.shape[2] - 1) // 2
    summed = jnp.zeros((half_rows, weight.shape[3], half_cols), jnp.float32)
    for row_tap in range(3):
        for col_tap in range(3):
            tap_segment = padded[
                row_tap : row_tap + 2 * half_rows : 2, :, col_tap : col_tap + 2 * half_cols : 2
            ]
            summed = summed + jnp.einsum(
                "cft,fg->cgt",
                tap_segment,
                weight[row_tap, col_tap],
                preferred_element_type=jnp.float32,
            )
    return summed


def conv_up(grad_ext, weight, half_rows, half_cols):
    parity_taps = {0: [(1, 0)], 1: [(0, 1), (2, 0)]}
    blocks = []
    for row_parity in (0, 1):
        inner_list = []
        for col_parity in (0, 1):
            summed = jnp.zeros((half_rows, weight.shape[2], half_cols), jnp.float32)
            for row_tap, row_skip in parity_taps[row_parity]:
                for col_tap, col_skip in parity_taps[col_parity]:
                    tap_segment = grad_ext[
                        row_skip : row_skip + half_rows, :, col_skip : col_skip + half_cols
                    ]
                    summed = summed + jnp.einsum(
                        "cgt,fg->cft",
                        tap_segment,
                        weight[row_tap, col_tap],
                        preferred_element_type=jnp.float32,
                    )
            inner_list.append(summed)
        blocks.append(jnp.stack(inner_list, axis=-1))
    stacked = jnp.stack(blocks, axis=1)
    return stacked.reshape(2 * half_rows, weight.shape[2], 2 * half_cols)


def conv_grad(padded, grad_block):
    half_rows = grad_block.shape[0]
    half_cols = grad_block.shape[2]
    rows_list = []
    for row_tap in range(3):
        cols_list = []
        for col_tap in range(3):
            tap_segment = padded[
                row_tap : row_tap + 2 * half_rows : 2, :, col_tap : col_tap + 2 * half_cols : 2
            ]
            cols_list.append(
                jnp.einsum(
                    "cft,cgt->fg", tap_segment, grad_block, preferred_element_type=jnp.float32
                )
            )
        rows_list.append(jnp.stack(cols_list, axis=0))
    return jnp.stack(rows_list, axis=0)


def gelu_back(pre_act, upstream):
    unused_value, pullback = jax.vjp(jax.nn.gelu, pre_act)
    return pullback(upstream)[0]


def local(signal, depth_weight, point_weight, conv_weight, grad_out):
    channels, features, sample_values = signal.shape
    extended_signal = extended(signal, (("tm", 2),), RIM)
    depth_low = depthwise(extended_signal, depth_weight, sample_values).astype(jnp.bfloat16)
    mixed_pre = jnp.einsum(
        "cft,fg->cgt", depth_low, point_weight, preferred_element_type=jnp.float32
    )
    hidden = (signal.astype(jnp.float32) + jax.nn.gelu(mixed_pre)).astype(jnp.bfloat16)
    upper_row = passed_along(hidden[channels - 1 :], "chan", 1)
    with_row = jnp.concatenate([upper_row, hidden], axis=0)
    corner_col = passed_along(with_row[:, :, sample_values - 1 :], "tm", 1)
    padded = jnp.concatenate([corner_col, with_row], axis=2)
    features_out = conv_down(padded, conv_weight).astype(jnp.bfloat16)
    lower_row = passed_along(grad_out[:1], "chan", -1)
    grad_rows = jnp.concatenate([grad_out, lower_row], axis=0)
    right_col = passed_along(grad_rows[:, :, :1], "tm", -1)
    grad_ext = jnp.concatenate([grad_rows, right_col], axis=2)
    grad_hidden = conv_up(grad_ext, conv_weight, grad_out.shape[0], grad_out.shape[2])
    conv_local = conv_grad(padded, grad_out)
    grad_mixed = gelu_back(mixed_pre, grad_hidden).astype(jnp.bfloat16)
    point_local = jnp.einsum(
        "cft,cgt->fg", depth_low, grad_mixed, preferred_element_type=jnp.float32
    )
    grad_depth_out = jnp.einsum(
        "cgt,fg->cft", grad_mixed, point_weight, preferred_element_type=jnp.float32
    )
    grad_depth_ext = extended(grad_depth_out, (("tm", 2),), RIM)
    depth_list = []
    for kernel_tap_index in range(KERNEL_TAPS):
        tap_segment = extended_signal[
            :,
            :,
            kernel_tap_index * DILATION_STEP : kernel_tap_index * DILATION_STEP + sample_values,
        ].astype(jnp.float32)
        depth_list.append(jnp.sum(tap_segment * grad_depth_out, axis=(0, 2)))
    depth_local = jnp.stack(depth_list, axis=1)
    grad_signal = grad_hidden
    for kernel_tap_index in range(KERNEL_TAPS):
        start_offset = (KERNEL_TAPS - 1 - kernel_tap_index) * DILATION_STEP
        grad_signal = (
            grad_signal
            + depth_weight[:, kernel_tap_index][None, :, None]
            * grad_depth_ext[:, :, start_offset : start_offset + sample_values]
        )
    reduced = lax.psum((depth_local, point_local, conv_local), ("chan", "tm"))
    return (features_out, grad_signal.astype(jnp.bfloat16), reduced[0], reduced[1], reduced[2])


def solution(mesh):
    in_specs = (P("chan", None, "tm"), P(), P(), P(), P("chan", None, "tm"))
    out_specs = (P("chan", None, "tm"), P("chan", None, "tm"), P(), P(), P())
    return jax.shard_map(local, mesh=mesh, in_specs=in_specs, out_specs=out_specs, check_vma=False)
```

profile of v0, /device:TPU:1, one launch (start us, length us, event | category | flops | bytes accessed | tf_op | source)
XLA Modules:
  0.0 515.1 jit_solution(8390581558329988342)
XLA Ops:
  7.2 0.8 slice.224
  8.1 5.2 %collective-permute-start.4 = (bf16[1,64,256]{2,1,0:T(8,128)(2,1)S(1)}, bf16[1,64,256]{2,1,0:T(8,128)(2,1)S(1)}, u32[]{:S(2)}, u32[]{:S(2)}) collective-permute-start(bf16[1,64,256]{2,1,0:T(8,128)(2,1)S(1)} %slice.224), channel_id=1, source_target_pairs={{16,0},{32,16},{48,32},{64,48},{80,64},{96,80},{112,96},{128,112},... | collective-permute-start | bytes 98312 | tf_op jit(solution)/shard_map/ppermute | solution.py:27
  13.3 1.9 fusion.111
  15.2 1.3 collective-permute-start.1
  16.5 4.0 collective-permute-start
  20.5 1.2 convolution_bitcast_fusion.3
  21.7 0.9 convolution_bitcast_fusion.4
  23.6 1.3 collective-permute-start.5
  25.1 5.8 %collective-permute-done.5 = bf16[9,64,1]{2,1,0:T(8,128)(2,1)S(1)} collective-permute-done((bf16[9,64,1]{2,1,0:T(8,128)(2,1)S(1)}, bf16[9,64,1]{2,1,0:T(8,128)(2,1)S(1)}, u32[]{:S(2)}, u32[]{:S(2)}) %collective-permute-start.5) | collective-permute-done | bytes 1184 | tf_op jit(solution)/shard_map/ppermute | solution.py:27
  32.2 1.5 pad_maximum_fusion.2
  33.7 6.7 %copy.49 = f32[8,2,64,256,2]{2,4,3,1,0:T(2,128)} copy(f32[8,2,64,256,2]{3,2,0,4,1:T(8,128)} %pad_maximum_fusion.2) | data formatting | bytes 4194304 | tf_op jit(solution)/shard_map/stack | solution.py:80
  40.4 3.8 copy.52
  44.2 1.0 constant_dynamic-update-slice_fusion
  45.3 2.6 fusion.6
  47.9 3.0 fusion.35
  51.5 9.5 %slice.222 = bf16[8,64,256]{2,1,0:T(8,128)(2,1)S(1)} slice(bf16[16,64,512]{2,1,0:T(8,128)(2,1)S(1)} %get-tuple-element.21), slice={[1:16:2], [0:64:1], [1:512:2]} | slice | bytes 524288 | tf_op jit(solution)/shard_map/slice | solution.py:48
  61.0 9.5 %slice.220 = bf16[8,64,256]{2,1,0:T(8,128)(2,1)S(1)} slice(bf16[16,64,512]{2,1,0:T(8,128)(2,1)S(1)} %get-tuple-element.21), slice={[1:16:2], [0:64:1], [0:512:2]} | slice | bytes 524288 | tf_op jit(solution)/shard_map/slice | solution.py:48
  70.5 10.0 %slice.216 = bf16[8,64,256]{2,1,0:T(8,128)(2,1)} slice(bf16[16,64,512]{2,1,0:T(8,128)(2,1)S(1)} %get-tuple-element.21), slice={[0:16:2], [0:64:1], [1:512:2]} | slice | bytes 524288 | tf_op jit(solution)/shard_map/slice | solution.py:48
  80.5 9.3 %slice.214 = bf16[8,64,256]{2,1,0:T(8,128)(2,1)S(1)} slice(bf16[16,64,512]{2,1,0:T(8,128)(2,1)S(1)} %get-tuple-element.21), slice={[0:16:2], [0:64:1], [0:512:2]} | slice | bytes 524288 | tf_op jit(solution)/shard_map/slice | solution.py:48
  90.1 1.9 fusion.72
  92.2 1.8 fusion.64
  94.0 2.3 collective-permute-start.2
  96.3 0.8 convolution_bitcast_fusion.8
  97.4 3.0 fusion.12
  100.4 1.1 fusion.110
  101.5 0.8 copy-done.10
  102.8 1.4 collective-permute-start.6
  104.2 4.8 collective-permute-start.7
  109.1 89.1 %all-reduce = (f32[64,7]{0,1:T(8,128)}, f32[64,64]{1,0:T(8,128)}) all-reduce(f32[64,7]{0,1:T(8,128)S(1)} %stack.115, f32[64,64]{1,0:T(8,128)S(1)} %convolution_bitcast_fusion.7), channel_id=1, replica_groups=mesh['chan'=16,'tm'=16] {'chan','tm'}, use_global_device_ids=true, to_apply=%region_7.0 | all-reduce | flops 4544 | bytes 36352 | tf_op jit(solution)/shard_map/psum | solution.py:152
  198.3 9.3 %slice.210 = bf16[8,64,256]{2,1,0:T(8,128)(2,1)S(1)} slice(bf16[17,64,512]{2,1,0:T(8,128)(2,1)S(1)} %pad_maximum_fusion.3), slice={[0:16:2], [0:64:1], [1:512:2]} | slice | bytes 524288 | tf_op jit(solution)/shard_map/slice | solution.py:48
  207.7 9.3 %slice.208 = bf16[8,64,256]{2,1,0:T(8,128)(2,1)S(1)} slice(bf16[17,64,512]{2,1,0:T(8,128)(2,1)S(1)} %pad_maximum_fusion.3), slice={[0:16:2], [0:64:1], [0:512:2]} | slice | bytes 524288 | tf_op jit(solution)/shard_map/slice | solution.py:48
  217.0 0.8 convolution_bitcast_fusion.15
  217.8 1.1 fusion.82
  219.1 1.5 collective-permute-start.3
  220.6 1.1 fusion.79
  221.6 0.8 convolution_bitcast_fusion.14
  222.5 3.4 collective-permute-done.3
  225.9 0.8 maximum_maximum_fusion
  226.7 9.5 %slice.218 = bf16[8,64,256]{2,1,0:T(8,128)(2,1)S(1)} slice(bf16[17,64,513]{2,1,0:T(8,128)(2,1)S(1)} %maximum_maximum_fusion), slice={[2:17:2], [0:64:1], [0:512:2]} | slice | bytes 524288 | tf_op jit(solution)/shard_map/slice | solution.py:48
  236.2 9.4 %slice.212 = bf16[8,64,256]{2,1,0:T(8,128)(2,1)S(1)} slice(bf16[17,64,513]{2,1,0:T(8,128)(2,1)S(1)} %maximum_maximum_fusion), slice={[1:17:2], [0:64:1], [0:512:2]} | slice | bytes 524288 | tf_op jit(solution)/shard_map/slice | solution.py:48
  245.6 9.3 %slice.206 = bf16[8,64,256]{2,1,0:T(8,128)(2,1)S(1)} slice(bf16[17,64,513]{2,1,0:T(8,128)(2,1)S(1)} %maximum_maximum_fusion), slice={[0:16:2], [0:64:1], [0:512:2]} | slice | bytes 524288 | tf_op jit(solution)/shard_map/slice | solution.py:48
  255.2 1.0 fusion.75
  256.7 0.8 maximum_bitcast_fusion.2
  257.5 0.7 pad_maximum_fusion.5
  259.6 1.0 fusion.55
  260.9 7.1 %fusion.17 = bf16[16,64,512]{2,1,0:T(8,128)(2,1)} fusion(f32[16,64,512]{2,1,0:T(8,128)S(1)} %copy-done.8, f32[16,64,512]{2,1,0:T(8,128)S(1)} %copy-done.3, f32[16,64,24]{2,1,0:T(8,128)} %collective-permute-done.7, f32[16,64,24]{2,1,0:T(8,128)} %collective-permute-done.6, f32[64]{0:T(128)S(1)} %copy-done.36, f32[64]{0:T(128)S(1)} %copy-done.38, ...), kind=kLoop, calls=%fused_computation.42 | loop fusion | flops 11010048 | bytes 5441280 | tf_op jit(solution)/shard_map/convert_element_type | solution.py:153
  268.0 238.6 %all-reduce.3.cloned.1.call-done = f32[3,3,64,64]{3,2,1,0:T(8,128)} async-done(((f32[3,3,64,64]{3,2,1,0:T(8,128)}), f32[3,3,64,64]{3,2,1,0:T(8,128)}) %all-reduce.3.cloned.1.call-update) | async-done | bytes 147472 | tf_op jit(solution)/shard_map/psum | solution.py:152
  506.6 1.7 copy.85
  (116 shorter events, 6.5 us)
Async XLA Ops:
  7.2 40.7 %copy-start = (bf16[64,64]{1,0:T(8,128)(2,1)S(1)}, bf16[64,64]{1,0:T(8,128)(2,1)}, u32[]{:S(2)}) copy-start(bf16[64,64]{1,0:T(8,128)(2,1)} %param.7) | copy-start | bytes 24580
  7.2 14.5 %copy-start.1 = (bf16[8,64,256]{2,1,0:T(8,128)(2,1)S(1)}, bf16[8,64,256]{2,1,0:T(8,128)(2,1)}, u32[]{:S(2)}) copy-start(bf16[8,64,256]{2,1,0:T(8,128)(2,1)} %param.9) | copy-start | bytes 786436
  7.2 15.4 %copy-start.19 = (bf16[3,3,64,64]{3,2,1,0:T(8,128)(2,1)S(1)}, bf16[3,3,64,64]{3,2,1,0:T(8,128)(2,1)}, u32[]{:S(2)}) copy-start(bf16[3,3,64,64]{3,2,1,0:T(8,128)(2,1)} %param.8) | copy-start | bytes 221188
  7.2 499.4 %all-reduce.3.cloned.1.call-start = ((), (), s32[]{:S(2)}) async-start(), calls=%async_computation | async-start | bytes 589824 | tf_op jit(solution)/shard_map/psum | solution.py:152
  8.1 15.0 %copy-start.4 = (bf16[16,64,512]{2,1,0:T(8,128)(2,1)S(1)}, bf16[16,64,512]{2,1,0:T(8,128)(2,1)}, u32[]{:S(2)}) copy-start(bf16[16,64,512]{2,1,0:T(8,128)(2,1)} %param.5) | copy-start | bytes 3145732
  8.1 15.2 %collective-permute-start.4 = (bf16[1,64,256]{2,1,0:T(8,128)(2,1)S(1)}, bf16[1,64,256]{2,1,0:T(8,128)(2,1)S(1)}, u32[]{:S(2)}, u32[]{:S(2)}) collective-permute-start(bf16[1,64,256]{2,1,0:T(8,128)(2,1)S(1)} %slice.224), channel_id=1, source_target_pairs={{16,0},{32,16},{48,32},{64,48},{80,64},{96,80},{112,96},{128,112},... | collective-permute-start | bytes 98312 | tf_op jit(solution)/shard_map/ppermute | solution.py:27
  15.2 28.9 %collective-permute-start.1 = (bf16[16,64,24]{2,1,0:T(8,128)(2,1)}, bf16[16,64,24]{2,1,0:T(8,128)(2,1)}, u32[]{:S(2)}, u32[]{:S(2)}) collective-permute-start(bf16[16,64,24]{2,1,0:T(8,128)(2,1)} %get-tuple-element.22), channel_id=1, source_target_pairs={{1,0},{2,1},{3,2},{4,3},{5,4},{6,5},{7,6},{8,7},{9,8},{10,9},{11,1... | collective-permute-start | bytes 147464 | tf_op jit(solution)/shard_map/ppermute | solution.py:19
  16.5 28.7 %collective-permute-start = (bf16[16,64,24]{2,1,0:T(8,128)(2,1)}, bf16[16,64,24]{2,1,0:T(8,128)(2,1)S(1)}, u32[]{:S(2)}, u32[]{:S(2)}) collective-permute-start(bf16[16,64,24]{2,1,0:T(8,128)(2,1)} %get-tuple-element.23), channel_id=1, source_target_pairs={{0,1},{1,2},{2,3},{3,4},{4,5},{5,6},{6,7},{7,8},{8,9},{9,10},{10,1... | collective-permute-start | bytes 147464 | tf_op jit(solution)/shard_map/ppermute | solution.py:18
  21.7 1.5 copy-start.39
  23.2 22.0 %copy-start.25 = (f32[64]{0:T(128)}, f32[64]{0:T(128)S(1)}, u32[]{:S(2)}) copy-start(f32[64]{0:T(128)S(1)} %get-tuple-element.24) | copy-start | bytes 772
  23.2 22.0 %copy-start.27 = (f32[64]{0:T(128)}, f32[64]{0:T(128)S(1)}, u32[]{:S(2)}) copy-start(f32[64]{0:T(128)S(1)} %get-tuple-element.25) | copy-start | bytes 772
  23.2 22.0 %copy-start.29 = (f32[64]{0:T(128)}, f32[64]{0:T(128)S(1)}, u32[]{:S(2)}) copy-start(f32[64]{0:T(128)S(1)} %get-tuple-element.26) | copy-start | bytes 772
  23.2 22.0 %copy-start.31 = (f32[64]{0:T(128)}, f32[64]{0:T(128)S(1)}, u32[]{:S(2)}) copy-start(f32[64]{0:T(128)S(1)} %get-tuple-element.27) | copy-start | bytes 772
  23.2 22.0 %copy-start.33 = (f32[64]{0:T(128)}, f32[64]{0:T(128)S(1)}, u32[]{:S(2)}) copy-start(f32[64]{0:T(128)S(1)} %get-tuple-element.28) | copy-start | bytes 772
  23.2 22.0 %copy-start.35 = (f32[64]{0:T(128)}, f32[64]{0:T(128)S(1)}, u32[]{:S(2)}) copy-start(f32[64]{0:T(128)S(1)} %get-tuple-element.29) | copy-start | bytes 772
  23.3 22.0 %copy-start.37 = (f32[64]{0:T(128)}, f32[64]{0:T(128)S(1)}, u32[]{:S(2)}) copy-start(f32[64]{0:T(128)S(1)} %get-tuple-element.30) | copy-start | bytes 772
  23.6 7.4 %collective-permute-start.5 = (bf16[9,64,1]{2,1,0:T(8,128)(2,1)S(1)}, bf16[9,64,1]{2,1,0:T(8,128)(2,1)S(1)}, u32[]{:S(2)}, u32[]{:S(2)}) collective-permute-start(bf16[9,64,1]{2,1,0:T(8,128)(2,1)S(1)} %slice.247), channel_id=1, source_target_pairs={{1,0},{2,1},{3,2},{4,3},{5,4},{6,5},{7,6},{8,7},{9,8},{10,9},{11,1... | collective-permute-start | bytes 3464 | tf_op jit(solution)/shard_map/ppermute | solution.py:27
  45.2 2.7 copy-start.21
  45.3 2.6 copy-start.2
  45.3 2.6 copy-start.5
  47.9 3.0 copy-start.9
  89.8 7.3 %copy-start.11 = (bf16[8,64,256]{2,1,0:T(8,128)(2,1)S(1)}, bf16[8,64,256]{2,1,0:T(8,128)(2,1)}, u32[]{:S(2)}) copy-start(bf16[8,64,256]{2,1,0:T(8,128)(2,1)} %slice.216) | copy-start | bytes 786436
  89.8 7.5 %copy-start.6 = (bf16[16,64,512]{2,1,0:T(8,128)(2,1)S(1)}, bf16[16,64,512]{2,1,0:T(8,128)(2,1)}, u32[]{:S(2)}) copy-start(bf16[16,64,512]{2,1,0:T(8,128)(2,1)} %param.5) | copy-start | bytes 3145732
  89.8 7.5 %copy-start.18 = (bf16[16,64,512]{2,1,0:T(8,128)(2,1)S(1)}, bf16[16,64,512]{2,1,0:T(8,128)(2,1)}, u32[]{:S(2)}) copy-start(bf16[16,64,512]{2,1,0:T(8,128)(2,1)} %get-tuple-element.20) | copy-start | bytes 3145732
  89.9 7.5 %copy-start.22 = (bf16[16,64,24]{2,1,0:T(8,128)(2,1)S(1)}, bf16[16,64,24]{2,1,0:T(8,128)(2,1)}, u32[]{:S(2)}) copy-start(bf16[16,64,24]{2,1,0:T(8,128)(2,1)} %copy-done.21) | copy-start | bytes 147460
  94.0 104.2 %collective-permute-start.2 = (bf16[1,64,512]{2,1,0:T(8,128)(2,1)}, bf16[1,64,512]{2,1,0:T(8,128)(2,1)S(1)}, u32[]{:S(2)}, u32[]{:S(2)}) collective-permute-start(bf16[1,64,512]{2,1,0:T(8,128)(2,1)} %slice.244), channel_id=1, source_target_pairs={{0,16},{16,32},{32,48},{48,64},{64,80},{80,96},{96,112},{112,128},... | collective-permute-start | bytes 196616 | tf_op jit(solution)/shard_map/ppermute | solution.py:27
  100.4 2.4 copy-start.7
  100.4 2.0 copy-start.10
  102.8 115.1 %copy-start.20 = (bf16[3,3,64,64]{3,2,1,0:T(8,128)(2,1)S(1)}, bf16[3,3,64,64]{3,2,1,0:T(8,128)(2,1)}, u32[]{:S(2)}) copy-start(bf16[3,3,64,64]{3,2,1,0:T(8,128)(2,1)} %param.8) | copy-start | bytes 221188
  102.8 157.8 %collective-permute-start.6 = (f32[16,64,24]{2,1,0:T(8,128)}, f32[16,64,24]{2,1,0:T(8,128)}, u32[]{:S(2)}, u32[]{:S(2)}) collective-permute-start(f32[16,64,24]{2,1,0:T(8,128)} %get-tuple-element.18), channel_id=1, source_target_pairs={{1,0},{2,1},{3,2},{4,3},{5,4},{6,5},{7,6},{8,7},{9,8},{10,9},{11,1... | collective-permute-start | bytes 294920 | tf_op jit(solution)/shard_map/ppermute | solution.py:19
  104.2 156.4 %collective-permute-start.7 = (f32[16,64,24]{2,1,0:T(8,128)}, f32[16,64,24]{2,1,0:T(8,128)}, u32[]{:S(2)}, u32[]{:S(2)}) collective-permute-start(f32[16,64,24]{2,1,0:T(8,128)} %get-tuple-element.19), channel_id=1, source_target_pairs={{0,1},{1,2},{2,3},{3,4},{4,5},{5,6},{6,7},{7,8},{8,9},{9,10},{10,1... | collective-permute-start | bytes 294920 | tf_op jit(solution)/shard_map/ppermute | solution.py:18
  219.1 6.8 %collective-permute-start.3 = (bf16[17,64,1]{2,1,0:T(8,128)(2,1)S(1)}, bf16[17,64,1]{2,1,0:T(8,128)(2,1)S(1)}, u32[]{:S(2)}, u32[]{:S(2)}) collective-permute-start(bf16[17,64,1]{2,1,0:T(8,128)(2,1)S(1)} %fusion.58), channel_id=1, source_target_pairs={{0,1},{1,2},{2,3},{3,4},{4,5},{5,6},{6,7},{7,8},{8,9},{9,10},{10,1... | collective-permute-start | bytes 6536 | tf_op jit(solution)/shard_map/ppermute | solution.py:27
  226.7 30.0 %copy-start.23 = (f32[1,64,64]{2,1,0:T(8,128)S(1)}, f32[1,64,64]{2,1,0:T(8,128)}, u32[]{:S(2)}) copy-start(f32[1,64,64]{2,1,0:T(8,128)} %convolution_bitcast_fusion.8) | copy-start | bytes 49156
  226.7 30.0 %copy-start.24 = (f32[1,64,64]{2,1,0:T(8,128)S(1)}, f32[1,64,64]{2,1,0:T(8,128)}, u32[]{:S(2)}) copy-start(f32[1,64,64]{2,1,0:T(8,128)} %convolution_bitcast_fusion.15) | copy-start | bytes 49156
  254.9 3.4 copy-start.14
  254.9 3.4 copy-start.15
  254.9 3.4 copy-start.16
  256.2 2.1 copy-start.17
  256.7 1.9 copy-start.12
  258.6 2.0 copy-start.3
  258.6 2.3 copy-start.8
  258.7 2.2 copy-start.26
  258.7 2.2 copy-start.28
  258.7 2.2 copy-start.30
  258.7 2.2 copy-start.32
  258.7 2.2 copy-start.34
  258.7 2.2 copy-start.36
  258.7 2.2 copy-start.38
  (1 other events, 1.0 us)
Sparse Core Ops, SparseCore 0:
  258.4 248.1 all-reduce.2
where the time goes:
time: 516 us; the launch traced here: 515 us
  waiting for transfers between devices  248 us (48%)
  local copies, waits for them, and re-layouts  105 us (20%)
  blocking collectives  89.1 us (17%)
  matrix products  22.6 us (4%)
  starting transfers between devices  21.9 us (4%)
  between operations  14.9 us (3%)
  other arithmetic  14 us (3%)
    psum x1, waiting for transfers between devices, local(): reduced = lax.psum((depth_local, point_local, conv_local), ('chan', 'tm'))  239 us
    psum x1, blocking collectives, local(): reduced = lax.psum((depth_local, point_local, conv_local), ('chan', 'tm'))  89.1 us
    slice x9, local copies, waits for them, and re-layouts, conv_down(): padded[row_tap:row_tap + 2 * half_rows:2, :, col_tap:col_tap + 2 * half_c...  85.2 us
    ppermute x4, starting transfers between devices, passed_along(): return lax.ppermute(block, axis, route)  10.3 us
  transfers between devices with their start and end apart: 9, of which 3 were waited for; matrix products, arithmetic and copies ran while one was open for 17% of the time, Pallas kernels for 0%

commit v1 on v0

v1 whole, which is shorter than its diff:
```python
import functools
import math

import jax
import jax.numpy as jnp
from jax import lax
from jax.experimental import pallas as pl
from jax.experimental.pallas import tpu as pltpu
from jax.sharding import PartitionSpec as P

F32, BF16 = jnp.float32, jnp.bfloat16
MESH = pl.DeviceIdType.MESH
TAPS = 7
RIM = 24
EDGE = 48
EDGE_G = 16
PLANE_UNITS = 32
EXTRA_UNITS = 9


def dot(a, b):
    return lax.dot_general(a, b, (((1,), (0,)), ((), ())), preferred_element_type=F32)


def dot_nt(a, b):
    return lax.dot_general(a, b, (((1,), (1,)), ((), ())), preferred_element_type=F32)


def select_matrix(rows, cols, offset=0):
    r = lax.broadcasted_iota(jnp.int32, (rows, cols), 0)
    c = lax.broadcasted_iota(jnp.int32, (rows, cols), 1)
    return jnp.where(c == r + offset, 1.0, 0.0).astype(BF16)


def loop(lo, hi, body):
    def step(i, carry):
        body(i)
        return carry

    lax.fori_loop(lo, hi, step, 0)


def halo_kernel(
    n_chan, n_tm, sig_l, sig_r, sig_row, go_l, go_r, go_row,
    out_l, out_r, out_row, out_go,
    send_l, send_r, got_l, got_r, got_row, got_go, corner_l, corner_r, ssem, rsem,
):
    a, b = lax.axis_index("chan"), lax.axis_index("tm")
    up, down = lax.rem(a + 1, n_chan), lax.rem(a + n_chan - 1, n_chan)
    right, left = lax.rem(b + 1, n_tm), lax.rem(b + n_tm - 1, n_tm)
    around = [(a, left), (a, right), (up, b), (down, b), (up, left), (up, right), (down, left), (down, right)]
    barrier = pltpu.get_barrier_semaphore()
    for device in around:
        pl.semaphore_signal(barrier, inc=1, device_id=device, device_id_type=MESH)

    pick_sl, pick_sr = select_matrix(EDGE, 128), select_matrix(EDGE, 128, 128 - EDGE)
    pick_gl, pick_gr = select_matrix(EDGE_G, 128), select_matrix(EDGE_G, 128, 128 - EDGE_G)
    zero = jnp.zeros((64, 128), BF16)
    for m in range(-1, 8):
        if m >= 0:
            send_l[m + 1, 0:EDGE] = dot_nt(pick_sl, sig_l[m]).astype(BF16)
            send_r[m + 1, 0:EDGE] = dot_nt(pick_sr, sig_r[m]).astype(BF16)
        for pick, src, dst in ((pick_gl, go_l, send_l), (pick_gr, go_r, send_r)):
            low = src[m] if m >= 0 else zero
            high = src[m + 1] if m < 7 else zero
            pair = jnp.concatenate([low, high], axis=0)
            dst[m + 1, EDGE:] = dot_nt(pick, pair).astype(BF16)
    pl.semaphore_wait(barrier, len(around))

    pieces = [
        (send_l.at[pl.ds(1, 8)], got_r.at[pl.ds(1, 8)]),
        (send_r.at[pl.ds(1, 8)], got_l.at[pl.ds(1, 8)]),
        (sig_row.at[0], got_row),
        (go_row.at[0], got_go),
        (send_l.at[8, pl.ds(0, EDGE)], got_r.at[0, pl.ds(0, EDGE)]),
        (send_r.at[8, pl.ds(0, EDGE)], got_l.at[0, pl.ds(0, EDGE)]),
        (send_l.at[0, pl.ds(EDGE, EDGE_G)], corner_r),
        (send_r.at[0, pl.ds(EDGE, EDGE_G)], corner_l),
    ]
    copies = []
    for n in (2, 3, 4, 5, 6, 7, 0, 1):
        src, dst = pieces[n]
        copies.append(
            pltpu.make_async_remote_copy(
                src_ref=src, dst_ref=dst, send_sem=ssem.at[n], recv_sem=rsem.at[n],
                device_id=around[n], device_id_type=MESH,
            )
        )
        copies[-1].start()
    for copy in copies:
        copy.wait()

    first_a, last_a = (a > 0).astype(F32), (a < n_chan - 1).astype(F32)
    first_b, last_b = (b > 0).astype(F32), (b < n_tm - 1).astype(F32)
    for got, out, corner, inside in ((got_l, out_l, corner_l, first_b), (got_r, out_r, corner_r, last_b)):
        out[0, 0:EDGE] = (got[0, 0:EDGE].astype(F32) * (inside * first_a)).astype(BF16)
        out[0, EDGE:] = jnp.zeros((EDGE_G, 128), BF16)
        for n in range(1, 8):
            out[n] = (got[n].astype(F32) * inside).astype(BF16)
        out[8, 0:EDGE] = (got[8, 0:EDGE].astype(F32) * inside).astype(BF16)
        tail = got[8, EDGE:].astype(F32) + corner[...].astype(F32) * last_a
        out[8, EDGE:] = (tail * inside).astype(BF16)
    out_row[...] = (got_row[...].astype(F32) * first_a).astype(BF16)
    out_go[...] = (got_go[...].astype(F32) * last_a).astype(BF16)


def halo_exchange(signal, grad_out, n_chan, n_tm):
    pairs = signal.reshape(8, 128, 512)
    vm = lambda shape, where: pl.BlockSpec(shape, lambda i, where=where: where)
    shapes = [(9, 64, 128), (9, 64, 128), (64, 512), (64, 256)]
    return pl.pallas_call(
        functools.partial(halo_kernel, n_chan, n_tm),
        grid=(1,),
        out_shape=[jax.ShapeDtypeStruct(s, BF16) for s in shapes],
        in_specs=[
            vm((8, 128, 128), (0, 0, 0)),
            vm((8, 128, 128), (0, 0, 3)),
            vm((1, 64, 512), (15, 0, 0)),
            vm((8, 64, 128), (0, 0, 0)),
            vm((8, 64, 128), (0, 0, 1)),
            vm((1, 64, 256), (0, 0, 0)),
        ],
        out_specs=[vm(s, (0,) * len(s)) for s in shapes],
        scratch_shapes=[pltpu.VMEM((9, 64, 128), BF16)] * 4
        + [pltpu.VMEM((64, 512), BF16), pltpu.VMEM((64, 256), BF16)]
        + [pltpu.VMEM((EDGE_G, 128), BF16)] * 2
        + [pltpu.SemaphoreType.DMA((8,))] * 2,
        compiler_params=pltpu.CompilerParams(collective_id=0, has_side_effects=True),
        name="halo",
    )(pairs, pairs, signal, grad_out, grad_out, grad_out)


def compute_kernel(
    n_tm, sig, go, halo_l, halo_r, row, go_next, dw, pw, cw,
    feat, gsig, part,
    xt, gp, ht, hp, go_ext, gt, gh_s, ga, gb, gd, acc_c, acc_m, eye, wup, cwt, pw2, pwt2, wrow,
):
    b = lax.axis_index("tm")

    eye[...] = select_matrix(256, 256)
    lane = lax.broadcasted_iota(jnp.int32, (64, 128), 1)
    sub = lax.broadcasted_iota(jnp.int32, (64, 128), 0)
    twice = jnp.where(lax.rem(lane, 64) == sub, 1.0, 0.0)
    twice16 = twice.astype(BF16)
    r128 = lax.broadcasted_iota(jnp.int32, (128, 128), 0)
    c128 = lax.broadcasted_iota(jnp.int32, (128, 128), 1)
    same = (r128 < 64) == (c128 < 64)
    wide = dot(pw[...], twice16).astype(BF16)
    wide = jnp.concatenate([wide, wide], axis=0).astype(F32)
    pw2[...] = jnp.where(same, wide, 0.0).astype(BF16)
    eye64 = select_matrix(64, 64)
    turned = dot_nt(eye64, pw[...]).astype(BF16)
    turned = dot(turned, twice16)
    turned = jnp.concatenate([turned, turned], axis=0)
    pwt2[...] = jnp.where(same, turned, 0.0).astype(BF16)
    zero64 = jnp.zeros((64, 64), BF16)
    wup[128:256, 0:128] = jnp.zeros((128, 128), BF16)
    for j in range(3):
        first = dot_nt(eye64, jnp.concatenate([zero64, cw[0, j]], axis=0)).astype(BF16)
        rest = dot_nt(eye64, jnp.concatenate([cw[1, j], cw[2, j]], axis=0)).astype(BF16)
        cwt[:, j * 256 : j * 256 + 128] = first
        cwt[:, j * 256 + 128 : j * 256 + 256] = rest
        at = {1: (0, 0), 2: (0, 128), 0: (128, 128)}[j]
        wup[at[0] : at[0] + 64, at[1] : at[1] + 128] = rest
        wup[at[0] + 64 : at[0] + 128, at[1] : at[1] + 128] = first
    for k in range(TAPS):
        wrow[k : k + 1, :] = jnp.sum(twice * dw[:, k : k + 1], axis=0, keepdims=True)

    c0 = math.sqrt(2.0 / math.pi)

    def forward(n, x):
        unit = eye[...]
        xt[n, 48:304] = dot_nt(unit, x[:, 0:256])
        xt[n, 304:560] = dot_nt(unit, x[:, 256:512])
        xt[n, 0:48] = halo_l[n, 0:EDGE].astype(F32)
        xt[n, 560:608] = halo_r[n, 0:EDGE].astype(F32)
        low = wrow[0:1, :] * xt[n, 0:560]
        for k in range(1, TAPS):
            low = low + wrow[k : k + 1, :] * xt[n, 8 * k : 8 * k + 560]
        pre = dot(low.astype(BF16), pw2[...])
        sq = pre * pre
        th = jnp.tanh(c0 * (pre + 0.044715 * (sq * pre)))
        cdf = 0.5 * (1.0 + th)
        hidden = (xt[n, 24:584] + pre * cdf).astype(BF16)
        ht[n] = hidden.astype(F32)
        gp[n] = cdf + (0.5 * pre) * (1.0 - th * th) * (c0 + (3 * 0.044715 * c0) * sq)

    forward(0, jnp.concatenate([jnp.zeros((64, 512), BF16), row[...]], axis=0))
    loop(0, 8, lambda m: forward(m + 1, sig[m]))

    @pl.when(b == 0)
    def _():
        for n in range(9):
            ht[n, 23:24] = jnp.zeros((1, 128), F32)
            gp[n, 0:24] = jnp.zeros((24, 128), F32)

    @pl.when(b == n_tm - 1)
    def _():
        for n in range(9):
            gp[n, 536:560] = jnp.zeros((24, 128), F32)

    def split(n):
        for j in range(3):
            hp[j, n] = ht[n, pl.ds(23 + j, 256, stride=2), :].astype(BF16)

    loop(0, 9, split)

    go_ext[0:512] = go[...].reshape(512, 256)
    go_ext[512:576] = go_next[...]
    acc_c[...] = jnp.zeros_like(acc_c)
    acc_m[...] = jnp.zeros_like(acc_m)

    def down(o):
        taps = jnp.concatenate([hp[j, o + s] for j in range(3) for s in range(2)], axis=1)
        acc_c[...] += dot(go[o], taps)
        feat[o] = dot_nt(cwt[...], taps).astype(BF16)

    loop(0, 8, down)

    def backward(m):
        unit = eye[...]
        x = go_ext[pl.ds(pl.multiple_of(m * 64, 64), 128), :]
        gt[0:16] = halo_l[m + 1, EDGE:].astype(F32)
        gt[16:272] = dot_nt(unit, x)
        gt[272:288] = halo_r[m + 1, EDGE:].astype(F32)
        gt[288:296] = jnp.zeros((8, 128), F32)
        both = jnp.concatenate([gt[0:288].astype(BF16), gt[1:289].astype(BF16)], axis=1)
        grads = dot(both, wup[...])
        gh_s[pl.ds(0, 288, stride=2), :] = grads[:, 0:128]
        gh_s[pl.ds(1, 288, stride=2), :] = grads[:, 128:256]
        mixed = gh_s[8:568] * gp[m + 1]
        mixed16 = mixed.astype(BF16)
        ga[...] = mixed16
        gb[0:552] = mixed[8:560].astype(BF16)
        shifted = []
        for k in range(TAPS):
            at = 48 - 8 * k
            shifted.append(ga[at : at + 512] if k % 2 == 0 else gb[at - 8 : at + 504])
        acc_m[...] += dot(sig[m], jnp.concatenate(shifted, axis=1))
        gd[...] = dot(mixed16, pwt2[...])
        total = gh_s[32:544]
        for k in range(TAPS):
            at = 48 - 8 * k
            total = total + wrow[k : k + 1, :] * gd[at : at + 512]
        gsig[m] = dot_nt(unit[0:128, 0:128], total.astype(BF16)).astype(BF16)

    loop(0, 8, backward)

    part[0:64] = acc_c[:, 128:256]
    part[64:128] = acc_c[:, 384:512]
    part[128:192] = acc_c[:, 640:768]
    part[192:256] = jnp.where(lane < 64, pltpu.roll(acc_c[:, 0:128], 64, 1), acc_c[:, 256:384])
    point = jnp.zeros((64, 128), F32)
    depth = jnp.zeros((64, 128), F32)
    pw_wide = jnp.where(lane < 64, dot(pw[...], twice16), 0.0)
    for k in range(TAPS):
        tap = acc_m[0:64, k * 128 : k * 128 + 128] + pltpu.roll(
            acc_m[64:128, k * 128 : k * 128 + 128], 64, 1
        )
        point = point + dw[:, k : k + 1] * tap
        depth = depth + jnp.where(lane == k, jnp.sum(tap * pw_wide, axis=1, keepdims=True), 0.0)
    part[256:320] = jnp.where(lane < 64, point, acc_c[:, 512:640])
    square = jnp.concatenate([depth, jnp.zeros((64, 128), F32)], axis=0)
    part[320:328] = jnp.transpose(square)[0:8]


def local_compute(signal, grad_out, halos, depth_weight, point_weight, conv_weight, n_tm):
    whole = pl.BlockSpec(memory_space=pltpu.VMEM)
    feat, gsig, part = pl.pallas_call(
        functools.partial(compute_kernel, n_tm),
        out_shape=[
            jax.ShapeDtypeStruct((8, 64, 256), BF16),
            jax.ShapeDtypeStruct((8, 128, 512), BF16),
            jax.ShapeDtypeStruct((328, 128), F32),
        ],
        in_specs=[whole] * 9,
        out_specs=[whole] * 3,
        scratch_shapes=[
            pltpu.VMEM((9, 608, 128), F32),
            pltpu.VMEM((9, 560, 128), F32),
            pltpu.VMEM((9, 560, 128), F32),
            pltpu.VMEM((3, 9, 256, 128), BF16),
            pltpu.VMEM((576, 256), BF16),
            pltpu.VMEM((296, 128), F32),
            pltpu.VMEM((576, 128), F32),
            pltpu.VMEM((560, 128), BF16),
            pltpu.VMEM((560, 128), BF16),
            pltpu.VMEM((560, 128), F32),
            pltpu.VMEM((64, 768), F32),
            pltpu.VMEM((128, 896), F32),
            pltpu.VMEM((256, 256), BF16),
            pltpu.VMEM((256, 256), BF16),
            pltpu.VMEM((64, 768), BF16),
            pltpu.VMEM((128, 128), BF16),
            pltpu.VMEM((128, 128), BF16),
            pltpu.VMEM((8, 128), F32),
        ],
        compiler_params=pltpu.CompilerParams(vmem_limit_bytes=48 * 1024 * 1024),
        name="compute",
    )(signal.reshape(8, 128, 512), grad_out, *halos, depth_weight, point_weight, conv_weight)
    return feat, gsig.reshape(16, 64, 512), part


def sum_kernel(
    low_chan, low_tm, n_chan, n_tm, part, depth_out, point_out, conv_out,
    plane_in, plane_x, mine, tower_in, done, ssem, rsem, xssem, xrsem,
):
    a, b = lax.axis_index("chan"), lax.axis_index("tm")
    plane = low_chan * low_tm
    tower = (n_chan // low_chan) * (n_tm // low_tm)
    a_hi, b_hi = lax.div(a, low_chan), lax.div(b, low_tm)
    a_lo, b_lo = lax.rem(a, low_chan), lax.rem(b, low_tm)
    me = a_lo * low_tm + b_lo
    level = a_hi * (n_tm // low_tm) + b_hi
    per = PLANE_UNITS // plane

    def in_plane(d):
        p = lax.rem(me + d, plane)
        return p, (a_hi * low_chan + lax.div(p, low_tm), b_hi * low_tm + lax.rem(p, low_tm))

    def in_tower(d):
        q = lax.rem(level + d, tower)
        hi = n_tm // low_tm
        return q, (lax.div(q, hi) * low_chan + a_lo, lax.rem(q, hi) * low_tm + b_lo)

    barrier = pltpu.get_barrier_semaphore()

    def greet(d):
        pl.semaphore_signal(barrier, inc=1, device_id=in_plane(d)[1], device_id_type=MESH)

    def greet_tower(d):
        pl.semaphore_signal(barrier, inc=1, device_id=in_tower(d)[1], device_id_type=MESH)

    loop(1, plane, greet)
    loop(1, tower, greet_tower)
    pl.semaphore_wait(barrier, plane + tower - 2)

    def to_owner(d):
        p, device = in_plane(d)
        return pltpu.make_async_remote_copy(
            src_ref=part.at[pl.ds(p * per, per)], dst_ref=plane_in.at[d],
            send_sem=ssem.at[0, d], recv_sem=rsem.at[0, d], device_id=device, device_id_type=MESH,
        )

    def to_owner_x(d):
        p, device = in_plane(d)
        return pltpu.make_async_remote_copy(
            src_ref=part.at[PLANE_UNITS + lax.rem(p, EXTRA_UNITS)], dst_ref=plane_x.at[d],
            send_sem=xssem.at[0, d], recv_sem=xrsem.at[0, d], device_id=device, device_id_type=MESH,
        )

    def send(d):
        to_owner(d).start()

        @pl.when(in_plane(d)[0] < EXTRA_UNITS)
        def _():
            to_owner_x(d).start()

    loop(1, plane, send)
    own_x = me < EXTRA_UNITS

    loop(1, plane, lambda d: to_owner(d).wait_recv())
    total = part[pl.ds(me * per, per)]
    for d in range(1, plane):
        total = total + plane_in[d]
    mine[0:per] = total

    def tower_copy(d, src, dst, s, r):
        return pltpu.make_async_remote_copy(
            src_ref=src, dst_ref=dst, send_sem=s, recv_sem=r,
            device_id=in_tower(d)[1], device_id_type=MESH,
        )

    def to_level(d):
        return tower_copy(d, mine.at[pl.ds(0, per)], tower_in.at[level, pl.ds(0, per)], ssem.at[1, d], rsem.at[1, d])

    def to_level_x(d):
        return tower_copy(d, mine.at[per], tower_in.at[level, per], xssem.at[1, d], xrsem.at[1, d])

    loop(1, tower, lambda d: to_level(d).start())

    @pl.when(own_x)
    def _():
        loop(1, plane, lambda d: to_owner_x(d).wait_recv())
        total = part[PLANE_UNITS + me]
        for d in range(1, plane):
            total = total + plane_x[d]
        mine[per] = total
        loop(1, tower, lambda d: to_level_x(d).start())

    tower_in[level, 0:per] = mine[0:per]
    loop(1, tower, lambda d: to_level(d).wait_recv())
    total = tower_in[0, 0:per]
    for q in range(1, tower):
        total = total + tower_in[q, 0:per]
    done[pl.ds(me * per, per)] = total

    def spread(d):
        return pltpu.make_async_remote_copy(
            src_ref=done.at[pl.ds(me * per, per)], dst_ref=done.at[pl.ds(me * per, per)],
            send_sem=ssem.at[2, d], recv_sem=rsem.at[2, d],
            device_id=in_plane(d)[1], device_id_type=MESH,
        )

    def spread_x(d):
        at = PLANE_UNITS + lax.rem(me, EXTRA_UNITS)
        return pltpu.make_async_remote_copy(
            src_ref=done.at[at], dst_ref=done.at[at],
            send_sem=xssem.at[2, d], recv_sem=xrsem.at[2, d],
            device_id=in_plane(d)[1], device_id_type=MESH,
        )

    loop(1, plane, lambda d: spread(d).start())

    @pl.when(own_x)
    def _():
        tower_in[level, per] = mine[per]
        loop(1, tower, lambda d: to_level_x(d).wait_recv())
        total = tower_in[0, per]
        for q in range(1, tower):
            total = total + tower_in[q, per]
        done[PLANE_UNITS + me] = total
        loop(1, plane, lambda d: spread_x(d).start())

    loop(1, plane, lambda d: spread(d).wait_recv())

    def arrive_x(d):
        p = lax.rem(me + plane - d, plane)

        @pl.when(p < EXTRA_UNITS)
        def _():
            spread_x(d).wait_recv()

    loop(1, plane, arrive_x)

    def left_all(d):
        to_owner(d).wait_send()
        spread(d).wait_send()

        @pl.when(in_plane(d)[0] < EXTRA_UNITS)
        def _():
            to_owner_x(d).wait_send()

        @pl.when(own_x)
        def _():
            spread_x(d).wait_send()

    loop(1, plane, left_all)

    def left_tower(d):
        to_level(d).wait_send()

        @pl.when(own_x)
        def _():
            to_level_x(d).wait_send()

    loop(1, tower, left_tower)

    def tile(n):
        return done[n * 8 : n * 8 + 8].reshape(64, 128)

    zero = jnp.zeros((64, 128), F32)
    for n in range(5):
        turned = jnp.transpose(jnp.concatenate([tile(n), zero], axis=0))
        for half in range(2):
            if n < 3:
                at = (half + 1, n)
            elif n == 3:
                at = (0, half)
            elif half == 1:
                at = (0, 2)
            else:
                point_out[...] = tile(4)[:, 0:64]
                continue
            conv_out[at[0], at[1]] = turned[half * 64 : half * 64 + 64, 0:64]
    depth = jnp.concatenate([done[40], jnp.zeros((120, 128), F32)], axis=0)
    depth_out[...] = jnp.transpose(depth)[0:64, 0:TAPS]


def sum_all(part, n_chan, n_tm):
    low_chan, low_tm = (8, 4) if n_chan == 16 else (2, 2)
    plane = low_chan * low_tm
    tower = n_chan * n_tm // plane
    per = PLANE_UNITS // plane
    whole = pl.BlockSpec(memory_space=pltpu.VMEM)
    sems = pltpu.SemaphoreType.DMA((3, plane))
    return pl.pallas_call(
        functools.partial(sum_kernel, low_chan, low_tm, n_chan, n_tm),
        out_shape=[
            jax.ShapeDtypeStruct((64, TAPS), F32),
            jax.ShapeDtypeStruct((64, 64), F32),
            jax.ShapeDtypeStruct((3, 3, 64, 64), F32),
        ],
        in_specs=[whole],
        out_specs=[whole] * 3,
        scratch_shapes=[
            pltpu.VMEM((plane, per, 8, 128), F32),
            pltpu.VMEM((plane, 8, 128), F32),
            pltpu.VMEM((per + 1, 8, 128), F32),
            pltpu.VMEM((tower, per + 1, 8, 128), F32),
            pltpu.VMEM((PLANE_UNITS + EXTRA_UNITS, 8, 128), F32),
            sems, sems, sems, sems,
        ],
        compiler_params=pltpu.CompilerParams(collective_id=1, has_side_effects=True),
        name="sum_all",
    )(part.reshape(PLANE_UNITS + EXTRA_UNITS, 8, 128))


def solution(mesh):
    n_chan, n_tm = mesh.shape["chan"], mesh.shape["tm"]

    def local(signal, depth_weight, point_weight, conv_weight, grad_out):
        halos = halo_exchange(signal, grad_out, n_chan, n_tm)
        feat, gsig, part = local_compute(
            signal, grad_out, halos, depth_weight, point_weight, conv_weight, n_tm
        )
        depth, point, conv = sum_all(part, n_chan, n_tm)
        return feat, gsig, depth, point, conv

    in_specs = (P("chan", None, "tm"), P(), P(), P(), P("chan", None, "tm"))
    out_specs = (P("chan", None, "tm"), P("chan", None, "tm"), P(), P(), P())
    return jax.shard_map(local, mesh=mesh, in_specs=in_specs, out_specs=out_specs, check_vma=False)
```

time: 516 us -> 71.2 us (0.14)
  waiting for transfers between devices: 248 us -> 0 us
  local copies, waits for them, and re-layouts: 105 us -> 8.62 us
  blocking collectives: 89.1 us -> 0 us
  Pallas kernels: 0 us -> 61.4 us
  matrix products: 22.6 us -> 0 us
  starting transfers between devices: 21.9 us -> 0 us
  between operations: 14.9 us -> 0.73 us
  other arithmetic: 14 us -> 0 us
    psum x1 -> x0, waiting for transfers between devices: 239 us -> none  [local(): reduced = lax.psum((depth_local, point_local, conv_local), ('chan', 'tm'))]
    slice x14 -> x0, local copies, waits for them, and re-layouts: 89.7 us -> none  [the longest x9 85.2 us: conv_down(): padded[row_tap:row_tap + 2 * half_rows:2, :, col_tap:col_tap + 2 * half_c...]
    psum x1 -> x0, blocking collectives: 89.1 us -> none  [local(): reduced = lax.psum((depth_local, point_local, conv_local), ('chan', 'tm'))]
    pallas_call x0 -> x3, Pallas kernels: none -> 61.4 us  [the longest x1 26.6 us: sum_all(): pl.pallas_call(functools.partial(sum_kernel, low_chan, low_tm, n_chan, n_...]
    dot_general x30 -> x0, matrix products: 22.6 us -> none  [the longest x9 8.61 us: conv_down(): jnp.einsum('cft,fg->cgt', tap_segment, weight[row_tap, col_tap], preferre...]
    ppermute x8 -> x0, starting transfers between devices: 21.9 us -> none  [the longest x4 10.3 us: passed_along(): return lax.ppermute(block, axis, route)]
    convert_element_type x2 -> x0, other arithmetic: 9.66 us -> none  [the longest x1 7.09 us: local(): grad_signal.astype(jnp.bfloat16)]
    ppermute x8 -> x0, waiting for transfers between devices: 9.29 us -> none  [the longest x4 9.28 us: passed_along(): return lax.ppermute(block, axis, route)]
  transfers between devices with their start and end apart: 9 -> 0, of which waited for: 3 -> 0; matrix products, arithmetic and copies ran while one was open for 17% -> 0% of each run, Pallas kernels for 0% -> 0%
where the time goes in v1:
time: 71.2 us; the launch traced here: 70.7 us
  Pallas kernels  61.4 us (86%)
  local copies, waits for them, and re-layouts  8.62 us (12%)
  between operations  0.73 us (1%)
    pallas_call x1, Pallas kernels, sum_all(): pl.pallas_call(functools.partial(sum_kernel, low_chan, low_tm, n_chan, n_...  26.6 us
    pallas_call x1, Pallas kernels, halo_exchange(): pl.pallas_call(functools.partial(halo_kernel, n_chan, n_tm), grid=(1,), o...  18.9 us
    pallas_call x1, Pallas kernels, local_compute(): pl.pallas_call(functools.partial(compute_kernel, n_tm), out_shape=[jax.Sh...  15.9 us
    unnamed x24, local copies, waits for them, and re-layouts  8.62 us

profile of v1, /device:TPU:1, one launch (start us, length us, event | category | flops | bytes accessed | tf_op | source)
XLA Modules:
  0.0 70.7 jit_solution(2150716323671823387)
XLA Ops:
  0.6 0.8 %copy.10.dw = f32[64,7]{1,0:T(8,128)S(1)} copy(f32[64,7]{0,1:T(8,128)} %param.6) | data formatting | bytes 3584 | tf_op args[1]
  1.4 0.0 copy-start
  1.4 0.0 copy-start.1
  1.4 0.0 copy-start.3
  1.4 0.0 copy-start.8
  1.4 18.9 %halo.1 = (bf16[9,64,128]{2,1,0:T(8,128)(2,1)}, bf16[9,64,128]{2,1,0:T(8,128)(2,1)}, bf16[64,512]{1,0:T(8,128)(2,1)}, bf16[64,256]{1,0:T(8,128)(2,1)}) custom-call(bf16[8,128,512]{2,1,0:T(8,128)(2,1)} %bitcast.3, bf16[8,128,512]{2,1,0:T(8,128)(2,1)} %bitcast.4, bf16[16,64,512]{2,1,0:T(8,128)(2,1)} %sig_row.1, bf16[8,64,256]{2,1,0:T(8,128)(2,1)} %go.1, ...), custom_call_target="tpu_custom_call" | custom-call | tf_op jit(solution)/shard_map/halo/pallas_call | solution.py:111
  20.4 0.0 copy-done
  20.4 0.0 copy-done.1
  20.4 0.0 copy-done.3
  20.4 0.0 copy-done.8
  20.4 0.0 copy-start.4
  20.4 0.9 %copy-done.4 = bf16[9,64,128]{2,1,0:T(8,128)(2,1)S(1)} copy-done((bf16[9,64,128]{2,1,0:T(8,128)(2,1)S(1)}, bf16[9,64,128]{2,1,0:T(8,128)(2,1)}, u32[]{:S(2)}) %copy-start.4) | copy-done | bytes 147480
  21.3 0.0 copy-start.5
  21.3 0.9 %copy-done.5 = bf16[9,64,128]{2,1,0:T(8,128)(2,1)S(1)} copy-done((bf16[9,64,128]{2,1,0:T(8,128)(2,1)S(1)}, bf16[9,64,128]{2,1,0:T(8,128)(2,1)}, u32[]{:S(2)}) %copy-start.5) | copy-done | bytes 147480
  22.2 0.0 copy-start.6
  22.2 0.8 %copy-done.6 = bf16[64,512]{1,0:T(8,128)(2,1)S(1)} copy-done((bf16[64,512]{1,0:T(8,128)(2,1)S(1)}, bf16[64,512]{1,0:T(8,128)(2,1)}, u32[]{:S(2)}) %copy-start.6) | copy-done | bytes 65560
  23.1 0.0 copy-start.7
  23.1 0.8 %copy-done.7 = bf16[64,256]{1,0:T(8,128)(2,1)S(1)} copy-done((bf16[64,256]{1,0:T(8,128)(2,1)S(1)}, bf16[64,256]{1,0:T(8,128)(2,1)}, u32[]{:S(2)}) %copy-start.7) | copy-done | bytes 32792
  23.8 15.9 %compute.1 = (bf16[8,64,256]{2,1,0:T(8,128)(2,1)}, bf16[8,128,512]{2,1,0:T(8,128)(2,1)}, f32[328,128]{1,0:T(8,128)S(1)}) custom-call(bf16[8,128,512]{2,1,0:T(8,128)(2,1)S(1)} %bitcast.5, bf16[8,64,256]{2,1,0:T(8,128)(2,1)S(1)} %copy-done.1, bf16[9,64,128]{2,1,0:T(8,128)(2,1)S(1)} %copy-done.4, bf16[9,64,128]{2,1,0:T(8,128)(2,1)S(1)} %copy-done.5, ...), custom_call_target="tpu_custom_call" | custom-call | tf_op jit(solution)/shard_map/compute/pallas_call | solution.py:269
  39.7 0.0 copy-start.2
  39.7 0.7 copy-done.2
  40.4 26.6 %sum_all.1 = (f32[64,7]{1,0:T(8,128)}, f32[64,64]{1,0:T(8,128)}, f32[3,3,64,64]{3,2,1,0:T(8,128)}) custom-call(f32[41,8,128]{2,1,0:T(8,128)} %bitcast.6), custom_call_target="tpu_custom_call" | custom-call | tf_op jit(solution)/shard_map/sum_all/pallas_call | solution.py:487
  67.0 0.0 copy-start.9
  67.0 1.4 %copy.11 = f32[64,7]{0,1:T(8,128)} copy(f32[64,7]{1,0:T(8,128)} %get-tuple-element.27) | data formatting | bytes 3584
  68.4 0.0 copy-done.9
  68.4 0.6 copy.14
  69.0 1.7 %copy.15 = f32[3,3,64,64]{3,2,1,0:T(8,128)} copy(f32[3,3,64,64]{3,2,1,0:T(8,128)} %get-tuple-element.39) | data formatting | bytes 294912
Async XLA Ops:
  1.4 19.0 %copy-start = (bf16[16,64,512]{2,1,0:T(8,128)(2,1)S(1)}, bf16[16,64,512]{2,1,0:T(8,128)(2,1)}, u32[]{:S(2)}) copy-start(bf16[16,64,512]{2,1,0:T(8,128)(2,1)} %sig_row.1) | copy-start | bytes 3145732
  1.4 19.0 %copy-start.1 = (bf16[8,64,256]{2,1,0:T(8,128)(2,1)S(1)}, bf16[8,64,256]{2,1,0:T(8,128)(2,1)}, u32[]{:S(2)}) copy-start(bf16[8,64,256]{2,1,0:T(8,128)(2,1)} %go.1) | copy-start | bytes 786436
  1.4 19.0 %copy-start.3 = (bf16[3,3,64,64]{3,2,1,0:T(8,128)(2,1)S(1)}, bf16[3,3,64,64]{3,2,1,0:T(8,128)(2,1)}, u32[]{:S(2)}) copy-start(bf16[3,3,64,64]{3,2,1,0:T(8,128)(2,1)} %cw.1) | copy-start | bytes 221188
  1.4 19.0 %copy-start.8 = (bf16[64,64]{1,0:T(8,128)(2,1)S(1)}, bf16[64,64]{1,0:T(8,128)(2,1)}, u32[]{:S(2)}) copy-start(bf16[64,64]{1,0:T(8,128)(2,1)} %pw.1) | copy-start | bytes 24580
  20.4 0.9 %copy-start.4 = (bf16[9,64,128]{2,1,0:T(8,128)(2,1)S(1)}, bf16[9,64,128]{2,1,0:T(8,128)(2,1)}, u32[]{:S(2)}) copy-start(bf16[9,64,128]{2,1,0:T(8,128)(2,1)} %get-tuple-element.15.halo_l) | copy-start | bytes 442372
  21.3 0.9 %copy-start.5 = (bf16[9,64,128]{2,1,0:T(8,128)(2,1)S(1)}, bf16[9,64,128]{2,1,0:T(8,128)(2,1)}, u32[]{:S(2)}) copy-start(bf16[9,64,128]{2,1,0:T(8,128)(2,1)} %get-tuple-element.16.halo_r) | copy-start | bytes 442372
  22.2 0.8 %copy-start.6 = (bf16[64,512]{1,0:T(8,128)(2,1)S(1)}, bf16[64,512]{1,0:T(8,128)(2,1)}, u32[]{:S(2)}) copy-start(bf16[64,512]{1,0:T(8,128)(2,1)} %get-tuple-element.17.row) | copy-start | bytes 196612
  23.1 0.8 %copy-start.7 = (bf16[64,256]{1,0:T(8,128)(2,1)S(1)}, bf16[64,256]{1,0:T(8,128)(2,1)}, u32[]{:S(2)}) copy-start(bf16[64,256]{1,0:T(8,128)(2,1)} %get-tuple-element.18.go_next) | copy-start | bytes 98308
  39.7 0.7 copy-start.2
  67.0 1.4 %copy-start.9 = (f32[64,64]{1,0:T(8,128)S(1)}, f32[64,64]{1,0:T(8,128)}, u32[]{:S(2)}) copy-start(f32[64,64]{1,0:T(8,128)} %get-tuple-element.38) | copy-start | bytes 49156

commit v2 on v0

v2 whole, which is shorter than its diff:
```python
import functools
import math

import jax
import jax.numpy as jnp
from jax import lax
from jax.experimental import pallas as pl
from jax.experimental.pallas import tpu as pltpu
from jax.sharding import PartitionSpec as P

F32, BF16 = jnp.float32, jnp.bfloat16
MESH = pl.DeviceIdType.MESH
TAPS = 7
RIM = 24
EDGE = 48
EDGE_G = 16
PLANE_UNITS = 32
EXTRA_UNITS = 9


def dot(a, b):
    return lax.dot_general(a, b, (((1,), (0,)), ((), ())), preferred_element_type=F32)


def dot_nt(a, b):
    return lax.dot_general(a, b, (((1,), (1,)), ((), ())), preferred_element_type=F32)


def select_matrix(rows, cols, offset=0):
    r = lax.broadcasted_iota(jnp.int32, (rows, cols), 0)
    c = lax.broadcasted_iota(jnp.int32, (rows, cols), 1)
    return jnp.where(c == r + offset, 1.0, 0.0).astype(BF16)


def loop(lo, hi, body):
    def step(i, carry):
        body(i)
        return carry

    lax.fori_loop(lo, hi, step, 0)


C0 = math.sqrt(2.0 / math.pi)
C1 = 0.044715 * C0


def gelu_parts(pre):
    sq = pre * pre
    th = jnp.tanh(pre * (C0 + C1 * sq))
    cdf = 0.5 + 0.5 * th
    value = pre * cdf
    slope = cdf + value * (1.0 - cdf) * (2.0 * C0 + (6.0 * C1) * sq)
    return value, slope


def kernel(
    low_chan, low_tm, n_chan, n_tm,
    sig, go, dw, pw, cw,
    feat, gsig, depth_out, point_out, conv_out,
    send_l, send_r, halo_l, halo_r, row, corner_l, corner_r,
    xt, gp, ht, hp, go_ext, gt, gh_s, ga, gb, gd, acc_m, eye, wup, cwt, pw2, pwt2, wrow,
    part, plane_in, plane_x, mine, tower_in, done,
    hssem, hrsem, ssem, rsem, xssem, xrsem,
):
    a, b = lax.axis_index("chan"), lax.axis_index("tm")
    plane = low_chan * low_tm
    hi_tm = n_tm // low_tm
    tower = (n_chan // low_chan) * hi_tm
    per = PLANE_UNITS // plane
    a_hi, b_hi = lax.div(a, low_chan), lax.div(b, low_tm)
    a_lo, b_lo = lax.rem(a, low_chan), lax.rem(b, low_tm)
    me = a_lo * low_tm + b_lo
    level = a_hi * hi_tm + b_hi
    before_a, after_a = a > 0, a < n_chan - 1
    before_b, after_b = b > 0, b < n_tm - 1
    both_of = jnp.logical_and

    def in_plane(d):
        p = lax.rem(me + d, plane)
        return p, (a_hi * low_chan + lax.div(p, low_tm), b_hi * low_tm + lax.rem(p, low_tm))

    def in_tower(d):
        q = lax.rem(level + d, tower)
        return q, (lax.div(q, hi_tm) * low_chan + a_lo, lax.rem(q, hi_tm) * low_tm + b_lo)

    def owns_extra(p):
        return both_of(lax.rem(p, 3) == 0, p < 3 * EXTRA_UNITS)

    around = [
        ((a, b - 1), before_b, after_b),
        ((a, b + 1), after_b, before_b),
        ((a + 1, b), after_a, before_a),
        ((a - 1, b), before_a, after_a),
        ((a + 1, b - 1), both_of(after_a, before_b), both_of(before_a, after_b)),
        ((a + 1, b + 1), both_of(after_a, after_b), both_of(before_a, before_b)),
        ((a - 1, b - 1), both_of(before_a, before_b), both_of(after_a, after_b)),
        ((a - 1, b + 1), both_of(before_a, after_b), both_of(after_a, before_b)),
    ]
    barrier = pltpu.get_barrier_semaphore()
    greeted = plane + tower - 2
    for device, there, _ in around:
        greeted = greeted + there.astype(jnp.int32)

        @pl.when(there)
        def _(device=device):
            pl.semaphore_signal(barrier, inc=1, device_id=device, device_id_type=MESH)

    def greet(d):
        pl.semaphore_signal(barrier, inc=1, device_id=in_plane(d)[1], device_id_type=MESH)

    def greet_tower(d):
        pl.semaphore_signal(barrier, inc=1, device_id=in_tower(d)[1], device_id_type=MESH)

    loop(1, tower, greet_tower)
    loop(1, plane, greet)

    pick_s, pick_g = select_matrix(EDGE, 128), select_matrix(EDGE_G, 128)
    pick_sr, pick_gr = select_matrix(EDGE, 128, 128 - EDGE), select_matrix(EDGE_G, 128, 128 - EDGE_G)
    zero16 = jnp.zeros((64, 128), BF16)
    for m in range(-1, 8):
        for pick, pick2, lanes, glanes, dst in (
            (pick_s, pick_g, slice(0, 128), slice(0, 128), send_l),
            (pick_sr, pick_gr, slice(384, 512), slice(128, 256), send_r),
        ):
            if m >= 0:
                dst[m + 1, 0:EDGE] = dot_nt(pick, sig[m, :, lanes]).astype(BF16)
            low = go[m, :, glanes] if m >= 0 else zero16
            high = go[m + 1, :, glanes] if m < 7 else zero16
            dst[m + 1, EDGE:] = dot_nt(pick2, jnp.concatenate([low, high], axis=0)).astype(BF16)

    eye[...] = select_matrix(256, 256)
    lane = lax.broadcasted_iota(jnp.int32, (64, 128), 1)
    sub = lax.broadcasted_iota(jnp.int32, (64, 128), 0)
    twice16 = jnp.where(lax.rem(lane, 64) == sub, 1.0, 0.0).astype(BF16)
    r128 = lax.broadcasted_iota(jnp.int32, (128, 128), 0)
    c128 = lax.broadcasted_iota(jnp.int32, (128, 128), 1)
    same = (r128 < 64) == (c128 < 64)
    wide = dot(pw[...], twice16)
    pw2[...] = jnp.where(same, jnp.concatenate([wide, wide], axis=0), 0.0).astype(BF16)
    eye64 = select_matrix(64, 64)
    turned = dot(dot_nt(eye64, pw[...]).astype(BF16), twice16)
    pwt2[...] = jnp.where(same, jnp.concatenate([turned, turned], axis=0), 0.0).astype(BF16)
    zero64 = jnp.zeros((64, 64), BF16)
    wup[128:256, 0:128] = jnp.zeros((128, 128), BF16)
    for j in range(3):
        first = dot_nt(eye64, jnp.concatenate([zero64, cw[0, j]], axis=0)).astype(BF16)
        rest = dot_nt(eye64, jnp.concatenate([cw[1, j], cw[2, j]], axis=0)).astype(BF16)
        cwt[:, j * 256 : j * 256 + 128] = first
        cwt[:, j * 256 + 128 : j * 256 + 256] = rest
        at = {1: (0, 0), 2: (0, 128), 0: (128, 128)}[j]
        wup[at[0] : at[0] + 64, at[1] : at[1] + 128] = rest
        wup[at[0] + 64 : at[0] + 128, at[1] : at[1] + 128] = first
    wrow[0:TAPS, 0:64] = dw[...]
    wrow[0:TAPS, 64:128] = dw[...]
    wrow[TAPS:, :] = jnp.zeros((1, 128), F32)

    def turn(n, x):
        unit = eye[...]
        xt[n, 48:304] = dot_nt(unit, x[:, 0:256])
        xt[n, 304:560] = dot_nt(unit, x[:, 256:512])

    loop(0, 4, lambda i: [turn(2 * i + s + 1, sig[2 * i + s]) for s in range(2)] and None)
    go_ext[0:512] = go[...].reshape(512, 256)

    pl.semaphore_wait(barrier, greeted)
    pieces = [
        (send_l.at[pl.ds(1, 8)], halo_r.at[pl.ds(1, 8)]),
        (send_r.at[pl.ds(1, 8)], halo_l.at[pl.ds(1, 8)]),
        (sig.at[7, pl.ds(64, 64)], row),
        (go.at[0], go_ext.at[pl.ds(512, 64)]),
        (send_l.at[8, pl.ds(0, EDGE)], halo_r.at[0, pl.ds(0, EDGE)]),
        (send_r.at[8, pl.ds(0, EDGE)], halo_l.at[0, pl.ds(0, EDGE)]),
        (send_l.at[0, pl.ds(EDGE, EDGE_G)], corner_r),
        (send_r.at[0, pl.ds(EDGE, EDGE_G)], corner_l),
    ]
    copies = [
        pltpu.make_async_remote_copy(
            src_ref=src, dst_ref=dst, send_sem=hssem.at[n], recv_sem=hrsem.at[n],
            device_id=around[n][0], device_id_type=MESH,
        )
        for n, (src, dst) in enumerate(pieces)
    ]
    for n in (2, 3, 0, 1, 4, 5, 6, 7):

        @pl.when(around[n][1])
        def _(n=n):
            copies[n].start()

    def arrive(n):
        dst = pieces[n][1]

        @pl.when(around[n][2])
        def _():
            copies[n].wait_recv()

        @pl.when(jnp.logical_not(around[n][2]))
        def _():
            dst[...] = jnp.zeros(dst.shape, BF16)

    def taps(n, lo, count):
        low = wrow[0:1, :] * xt[n, lo : lo + count]
        for k in range(1, TAPS):
            low = low + wrow[k : k + 1, :] * xt[n, lo + 8 * k : lo + 8 * k + count]
        return low.astype(BF16)

    def forward(n, lo, count, with_slope=True):
        value, slope = gelu_parts(dot(taps(n, lo, count), pw2[...]))
        ht[n, lo : lo + count] = (xt[n, lo + 24 : lo + 24 + count] + value).astype(BF16).astype(F32)
        if with_slope:
            gp[n, lo : lo + count] = slope

    loop(1, 9, lambda n: forward(n, 48, 464))
    arrive(0)
    arrive(1)
    for lo, src, at in ((0, halo_l, 0), (512, halo_r, 560)):
        for n in range(1, 9):
            xt[n, at : at + EDGE] = src[n, 0:EDGE].astype(F32)
        pre = dot(jnp.concatenate([taps(n, lo, 48) for n in range(1, 9)], axis=0), pw2[...])
        value, slope = gelu_parts(pre)
        for n in range(1, 9):
            mine_rows = slice((n - 1) * 48, n * 48)
            x = xt[n, lo + 24 : lo + 72]
            ht[n, lo : lo + 48] = (x + value[mine_rows]).astype(BF16).astype(F32)
            gp[n, lo : lo + 48] = slope[mine_rows]
    arrive(2)
    arrive(4)
    arrive(5)
    xt[0, 0:EDGE] = halo_l[0, 0:EDGE].astype(F32)
    turn(0, jnp.concatenate([jnp.zeros((64, 512), BF16), row[...]], axis=0))
    xt[0, 560:608] = halo_r[0, 0:EDGE].astype(F32)
    forward(0, 16, 528, False)

    @pl.when(b == 0)
    def _():
        for n in range(9):
            ht[n, 23:24] = jnp.zeros((1, 128), F32)
            gp[n, 0:24] = jnp.zeros((24, 128), F32)

    @pl.when(b == n_tm - 1)
    def _():
        for n in range(9):
            gp[n, 536:560] = jnp.zeros((24, 128), F32)

    for n in range(9):
        for j in range(3):
            hp[j, n] = ht[n, pl.ds(23 + j, 256, stride=2), :].astype(BF16)

    grads = []
    for j in range(3):
        total = jnp.zeros((64, 256), F32)
        for o in range(8):
            total = total + dot(go[o], jnp.concatenate([hp[j, o], hp[j, o + 1]], axis=1))
        grads.append(total)
        put(part, 8 * j, total[:, 128:256])
    put(part, 24, jnp.where(lane < 64, pltpu.roll(grads[0][:, 0:128], 64, 1), grads[1][:, 0:128]))
    last = grads[2][:, 0:128]

    def remote(src, dst, s, r, device):
        return pltpu.make_async_remote_copy(
            src_ref=src, dst_ref=dst, send_sem=s, recv_sem=r, device_id=device, device_id_type=MESH
        )

    def to_owner(d):
        p, device = in_plane(d)
        return remote(part.at[pl.ds(p * per, per)], plane_in.at[d], ssem.at[0, d], rsem.at[0, d], device)

    def to_owner_x(d):
        p, device = in_plane(d)
        unit = PLANE_UNITS + lax.rem(lax.div(p, 3), EXTRA_UNITS)
        return remote(part.at[unit], plane_x.at[d], xssem.at[0, d], xrsem.at[0, d], device)

    def to_level(d):
        src, dst = mine.at[pl.ds(0, per)], tower_in.at[level, pl.ds(0, per)]
        return remote(src, dst, ssem.at[1, d], rsem.at[1, d], in_tower(d)[1])

    def to_level_x(d):
        return remote(mine.at[per], tower_in.at[level, per], xssem.at[1, d], xrsem.at[1, d], in_tower(d)[1])

    def spread(d):
        at = done.at[pl.ds(me * per, per)]
        return remote(at, at, ssem.at[2, d], rsem.at[2, d], in_plane(d)[1])

    own_x = owns_extra(me)
    unit_x = PLANE_UNITS + lax.rem(lax.div(me, 3), EXTRA_UNITS)

    def spread_x(d):
        at = done.at[unit_x]
        return remote(at, at, xssem.at[2, d], xrsem.at[2, d], in_plane(d)[1])

    loop(1, plane, lambda d: to_owner(d).start())

    arrive(3)
    arrive(6)
    arrive(7)
    for halo, corner in ((halo_l, corner_l), (halo_r, corner_r)):
        halo[8, EDGE:] = (halo[8, EDGE:].astype(F32) + corner[...].astype(F32)).astype(BF16)

    def backward(i):
        unit = eye[...]
        lhs, rhs = [], []
        for s in range(2):
            m = 2 * i + s
            x = go_ext[pl.ds(pl.multiple_of(m * 64, 64), 128), :]
            gt[s, 0:16] = halo_l[m + 1, EDGE:].astype(F32)
            gt[s, 16:272] = dot_nt(unit, x)
            gt[s, 272:288] = halo_r[m + 1, EDGE:].astype(F32)
            gt[s, 288:296] = jnp.zeros((8, 128), F32)
            both = jnp.concatenate([gt[s, 0:288].astype(BF16), gt[s, 1:289].astype(BF16)], axis=1)
            up = dot(both, wup[...])
            gh_s[m, pl.ds(0, 288, stride=2), :] = up[:, 0:128]
            gh_s[m, pl.ds(1, 288, stride=2), :] = up[:, 128:256]
            mixed = gh_s[m, 8:568] * gp[m + 1]
            ga[m] = mixed.astype(BF16)
            gb[s, 0:552] = mixed[8:560].astype(BF16)
            shifted = []
            for k in range(TAPS):
                at = 48 - 8 * k
                shifted.append(ga[m, at : at + 512] if k % 2 == 0 else gb[s, at - 8 : at + 504])
            lhs.append(sig[m])
            rhs.append(jnp.concatenate(shifted, axis=1))
        acc_m[...] += dot(jnp.concatenate(lhs, axis=1), jnp.concatenate(rhs, axis=0))

    acc_m[...] = jnp.zeros_like(acc_m)
    loop(0, 4, backward)

    point = jnp.zeros((64, 128), F32)
    depth = jnp.zeros((64, 128), F32)
    pw_wide = jnp.where(lane < 64, dot(pw[...], twice16), 0.0)
    dw_col = jnp.transpose(jnp.concatenate([wrow[...], jnp.zeros((120, 128), F32)], axis=0))
    for k in range(TAPS):
        tap = acc_m[0:64, k * 128 : k * 128 + 128] + pltpu.roll(
            acc_m[64:128, k * 128 : k * 128 + 128], 64, 1
        )
        point = point + dw_col[0:64, k : k + 1] * tap
        depth = depth + jnp.where(lane == k, jnp.sum(tap * pw_wide, axis=1, keepdims=True), 0.0)
    put(part, 32, jnp.where(lane < 64, point, last))
    square = jnp.concatenate([depth, jnp.zeros((64, 128), F32)], axis=0)
    part[40] = jnp.transpose(square)[0:8]

    def send_x(d):
        @pl.when(owns_extra(in_plane(d)[0]))
        def _():
            to_owner_x(d).start()

    loop(1, plane, send_x)

    for o in range(8):
        wide_taps = jnp.concatenate([hp[j, o + s] for j in range(3) for s in range(2)], axis=1)
        feat[o] = dot_nt(cwt[...], wide_taps).astype(BF16)

    loop(1, plane, lambda d: to_owner(d).wait_recv())
    total = part[pl.ds(me * per, per)]
    for d in range(1, plane):
        total = total + plane_in[d]
    mine[0:per] = total
    loop(1, tower, lambda d: to_level(d).start())

    def finish(i):
        unit = eye[0:128, 0:128]
        for s in range(2):
            m = 2 * i + s
            gd[s] = dot(ga[m], pwt2[...])
            total = gh_s[m, 32:544]
            for k in range(TAPS):
                at = 48 - 8 * k
                total = total + wrow[k : k + 1, :] * gd[s, at : at + 512]
            gsig[m] = dot_nt(unit, total.astype(BF16)).astype(BF16)

    loop(0, 2, finish)

    @pl.when(own_x)
    def _():
        loop(1, plane, lambda d: to_owner_x(d).wait_recv())
        total = part[unit_x]
        for d in range(1, plane):
            total = total + plane_x[d]
        mine[per] = total
        loop(1, tower, lambda d: to_level_x(d).start())

    tower_in[level, 0:per] = mine[0:per]
    loop(1, tower, lambda d: to_level(d).wait_recv())
    total = tower_in[0, 0:per]
    for q in range(1, tower):
        total = total + tower_in[q, 0:per]
    done[pl.ds(me * per, per)] = total
    loop(1, plane, lambda d: spread(d).start())

    loop(2, 4, finish)

    @pl.when(own_x)
    def _():
        tower_in[level, per] = mine[per]
        loop(1, tower, lambda d: to_level_x(d).wait_recv())
        total = tower_in[0, per]
        for q in range(1, tower):
            total = total + tower_in[q, per]
        done[unit_x] = total
        loop(1, plane, lambda d: spread_x(d).start())

    def tile(n):
        return done[n * 8 : n * 8 + 8].reshape(64, 128)

    def conv_tile(n):
        zero = jnp.zeros((64, 128), F32)
        return jnp.transpose(jnp.concatenate([tile(n), zero], axis=0))

    loop(1, plane, lambda d: spread(d).wait_recv())
    for n in range(4):
        turned = conv_tile(n)
        for half in range(2):
            i, j = (half + 1, n) if n < 3 else (0, half)
            conv_out[i, j] = turned[half * 64 : half * 64 + 64, 0:64]

    def arrive_x(d):
        @pl.when(owns_extra(lax.rem(me + plane - d, plane)))
        def _():
            spread_x(d).wait_recv()

    loop(1, plane, arrive_x)
    conv_out[0, 2] = conv_tile(4)[64:128, 0:64]
    point_out[...] = tile(4)[:, 0:64]
    depth_out[...] = done[40][0:TAPS, 0:64]

    for n in range(8):

        @pl.when(around[n][1])
        def _(n=n):
            copies[n].wait_send()

    def left_all(d):
        to_owner(d).wait_send()
        spread(d).wait_send()

        @pl.when(owns_extra(in_plane(d)[0]))
        def _():
            to_owner_x(d).wait_send()

        @pl.when(own_x)
        def _():
            spread_x(d).wait_send()

    loop(1, plane, left_all)

    def left_tower(d):
        to_level(d).wait_send()

        @pl.when(own_x)
        def _():
            to_level_x(d).wait_send()

    loop(1, tower, left_tower)


def put(ref, unit, tile):
    ref[unit : unit + 8] = tile.reshape(8, 8, 128)


def solution(mesh):
    n_chan, n_tm = mesh.shape["chan"], mesh.shape["tm"]
    low_chan, low_tm = 8, 4
    plane = low_chan * low_tm
    tower = n_chan * n_tm // plane
    per = PLANE_UNITS // plane
    whole = pl.BlockSpec(memory_space=pltpu.VMEM)
    sems = pltpu.SemaphoreType.DMA((3, plane))
    vm = pltpu.VMEM

    def local(signal, depth_weight, point_weight, conv_weight, grad_out):
        feat, gsig, depth, point, conv = pl.pallas_call(
            functools.partial(kernel, low_chan, low_tm, n_chan, n_tm),
            out_shape=[
                jax.ShapeDtypeStruct((8, 64, 256), BF16),
                jax.ShapeDtypeStruct((8, 128, 512), BF16),
                jax.ShapeDtypeStruct((TAPS, 64), F32),
                jax.ShapeDtypeStruct((64, 64), F32),
                jax.ShapeDtypeStruct((3, 3, 64, 64), F32),
            ],
            in_specs=[whole] * 5,
            out_specs=[whole] * 5,
            scratch_shapes=[
                vm((9, 64, 128), BF16),
                vm((9, 64, 128), BF16),
                vm((9, 64, 128), BF16),
                vm((9, 64, 128), BF16),
                vm((64, 512), BF16),
                vm((EDGE_G, 128), BF16),
                vm((EDGE_G, 128), BF16),
                vm((9, 608, 128), F32),
                vm((9, 560, 128), F32),
                vm((9, 560, 128), F32),
                vm((3, 9, 256, 128), BF16),
                vm((576, 256), BF16),
                vm((2, 296, 128), F32),
                vm((8, 576, 128), F32),
                vm((8, 560, 128), BF16),
                vm((2, 560, 128), BF16),
                vm((2, 560, 128), F32),
                vm((128, 896), F32),
                vm((256, 256), BF16),
                vm((256, 256), BF16),
                vm((64, 768), BF16),
                vm((128, 128), BF16),
                vm((128, 128), BF16),
                vm((8, 128), F32),
                vm((PLANE_UNITS + EXTRA_UNITS, 8, 128), F32),
                vm((plane, per, 8, 128), F32),
                vm((plane, 8, 128), F32),
                vm((per + 1, 8, 128), F32),
                vm((tower, per + 1, 8, 128), F32),
                vm((PLANE_UNITS + EXTRA_UNITS, 8, 128), F32),
                pltpu.SemaphoreType.DMA((8,)),
                pltpu.SemaphoreType.DMA((8,)),
                sems, sems, sems, sems,
            ],
            compiler_params=pltpu.CompilerParams(
                collective_id=0, has_side_effects=True, vmem_limit_bytes=48 * 1024 * 1024
            ),
            name="step",
        )(signal.reshape(8, 128, 512), grad_out, depth_weight.T, point_weight, conv_weight)
        return feat, gsig.reshape(16, 64, 512), depth.T, point, conv

    in_specs = (P("chan", None, "tm"), P(), P(), P(), P("chan", None, "tm"))
    out_specs = (P("chan", None, "tm"), P("chan", None, "tm"), P(), P(), P())
    return jax.shard_map(local, mesh=mesh, in_specs=in_specs, out_specs=out_specs, check_vma=False)
```

time: 516 us -> 53.1 us (0.10)
  waiting for transfers between devices: 248 us -> 0 us
  local copies, waits for them, and re-layouts: 105 us -> 8.07 us
  blocking collectives: 89.1 us -> 0 us
  Pallas kernels: 0 us -> 44.1 us
  matrix products: 22.6 us -> 0 us
  starting transfers between devices: 21.9 us -> 0 us
  between operations: 14.9 us -> 0.66 us
  other arithmetic: 14 us -> 0 us
    psum x1 -> x0, waiting for transfers between devices: 239 us -> none  [local(): reduced = lax.psum((depth_local, point_local, conv_local), ('chan', 'tm'))]
    slice x14 -> x0, local copies, waits for them, and re-layouts: 89.7 us -> none  [the longest x9 85.2 us: conv_down(): padded[row_tap:row_tap + 2 * half_rows:2, :, col_tap:col_tap + 2 * half_c...]
    psum x1 -> x0, blocking collectives: 89.1 us -> none  [local(): reduced = lax.psum((depth_local, point_local, conv_local), ('chan', 'tm'))]
    pallas_call x0 -> x1, Pallas kernels: none -> 44.1 us  [local(): pl.pallas_call(functools.partial(kernel, low_chan, low_tm, n_chan, n_tm),...]
    dot_general x30 -> x0, matrix products: 22.6 us -> none  [the longest x9 8.61 us: conv_down(): jnp.einsum('cft,fg->cgt', tap_segment, weight[row_tap, col_tap], preferre...]
    ppermute x8 -> x0, starting transfers between devices: 21.9 us -> none  [the longest x4 10.3 us: passed_along(): return lax.ppermute(block, axis, route)]
    convert_element_type x2 -> x0, other arithmetic: 9.66 us -> none  [the longest x1 7.09 us: local(): grad_signal.astype(jnp.bfloat16)]
    ppermute x8 -> x0, waiting for transfers between devices: 9.29 us -> none  [the longest x4 9.28 us: passed_along(): return lax.ppermute(block, axis, route)]
  transfers between devices with their start and end apart: 9 -> 0, of which waited for: 3 -> 0; matrix products, arithmetic and copies ran while one was open for 17% -> 0% of each run, Pallas kernels for 0% -> 0%
where the time goes in v2:
time: 53.1 us; the launch traced here: 52.8 us
  Pallas kernels  44.1 us (83%)
  local copies, waits for them, and re-layouts  8.07 us (15%)
  between operations  0.66 us (1%)
    pallas_call x1, Pallas kernels, local(): pl.pallas_call(functools.partial(kernel, low_chan, low_tm, n_chan, n_tm),...  44.1 us
    unnamed x15, local copies, waits for them, and re-layouts  8.07 us

profile of v2, /device:TPU:1, one launch (start us, length us, event | category | flops | bytes accessed | tf_op | source)
XLA Modules:
  0.0 52.8 jit_solution(16830632998987633222)
XLA Ops:
  0.6 0.0 copy-start
  0.6 1.2 %copy-done = bf16[16,64,512]{2,1,0:T(8,128)(2,1)S(1)} copy-done((bf16[16,64,512]{2,1,0:T(8,128)(2,1)S(1)}, bf16[16,64,512]{2,1,0:T(8,128)(2,1)}, u32[]{:S(2)}) %copy-start) | copy-done | bytes 1048600
  1.9 0.0 copy-start.1
  1.9 0.9 %copy-done.1 = bf16[8,64,256]{2,1,0:T(8,128)(2,1)S(1)} copy-done((bf16[8,64,256]{2,1,0:T(8,128)(2,1)S(1)}, bf16[8,64,256]{2,1,0:T(8,128)(2,1)}, u32[]{:S(2)}) %copy-start.1) | copy-done | bytes 262168
  2.8 0.0 copy-start.2
  2.8 0.9 %copy-done.2 = bf16[3,3,64,64]{3,2,1,0:T(8,128)(2,1)S(1)} copy-done((bf16[3,3,64,64]{3,2,1,0:T(8,128)(2,1)S(1)}, bf16[3,3,64,64]{3,2,1,0:T(8,128)(2,1)}, u32[]{:S(2)}) %copy-start.2) | copy-done | bytes 73752
  3.7 0.0 copy-start.3
  3.7 0.7 %copy-done.3 = bf16[64,64]{1,0:T(8,128)(2,1)S(1)} copy-done((bf16[64,64]{1,0:T(8,128)(2,1)S(1)}, bf16[64,64]{1,0:T(8,128)(2,1)}, u32[]{:S(2)}) %copy-start.3) | copy-done | bytes 8216
  4.4 0.0 copy-start.4
  4.4 0.7 %copy-done.4 = f32[64,7]{0,1:T(8,128)S(1)} copy-done((f32[64,7]{0,1:T(8,128)S(1)}, f32[64,7]{0,1:T(8,128)}, u32[]{:S(2)}) %copy-start.4) | copy-done | bytes 1816
  5.1 44.1 %step.1 = (bf16[8,64,256]{2,1,0:T(8,128)(2,1)S(1)}, bf16[8,128,512]{2,1,0:T(8,128)(2,1)S(1)}, f32[7,64]{1,0:T(8,128)S(1)}, f32[64,64]{1,0:T(8,128)S(1)}, f32[3,3,64,64]{3,2,1,0:T(8,128)S(1)}) custom-call(bf16[8,128,512]{2,1,0:T(8,128)(2,1)S(1)} %bitcast.4, bf16[8,64,256]{2,1,0:T(8,128)(2,1)S(1)} %copy-done.1, f32[7,64]{1,0:T(8,128)S(1)} %bitcast.6, ...), custom_call_target="tpu_custom_call" | custom-call | tf_op jit(solution)/shard_map/step/pallas_call | solution.py:469
  49.2 0.7 %copy.15 = bf16[8,64,256]{2,1,0:T(8,128)(2,1)} copy(bf16[8,64,256]{2,1,0:T(8,128)(2,1)S(1)} %get-tuple-element.20) | data formatting | bytes 524288
  50.0 1.0 %copy.16 = bf16[16,64,512]{2,1,0:T(8,128)(2,1)} copy(bf16[16,64,512]{2,1,0:T(8,128)(2,1)S(1)} %bitcast.5) | data formatting | bytes 2097152
  50.9 0.6 %copy.17 = f32[64,7]{0,1:T(8,128)} copy(f32[64,7]{0,1:T(8,128)S(1)} %bitcast.7) | data formatting | bytes 3584
  51.5 0.6 %copy.18 = f32[64,64]{1,0:T(8,128)} copy(f32[64,64]{1,0:T(8,128)S(1)} %get-tuple-element.23) | data formatting | bytes 32768
  52.1 0.7 %copy.19 = f32[3,3,64,64]{3,2,1,0:T(8,128)} copy(f32[3,3,64,64]{3,2,1,0:T(8,128)S(1)} %get-tuple-element.24) | data formatting | bytes 294912
Async XLA Ops:
  0.6 1.2 %copy-start = (bf16[16,64,512]{2,1,0:T(8,128)(2,1)S(1)}, bf16[16,64,512]{2,1,0:T(8,128)(2,1)}, u32[]{:S(2)}) copy-start(bf16[16,64,512]{2,1,0:T(8,128)(2,1)} %param.5) | copy-start | bytes 3145732
  1.9 0.9 %copy-start.1 = (bf16[8,64,256]{2,1,0:T(8,128)(2,1)S(1)}, bf16[8,64,256]{2,1,0:T(8,128)(2,1)}, u32[]{:S(2)}) copy-start(bf16[8,64,256]{2,1,0:T(8,128)(2,1)} %go.1) | copy-start | bytes 786436
  2.8 0.9 %copy-start.2 = (bf16[3,3,64,64]{3,2,1,0:T(8,128)(2,1)S(1)}, bf16[3,3,64,64]{3,2,1,0:T(8,128)(2,1)}, u32[]{:S(2)}) copy-start(bf16[3,3,64,64]{3,2,1,0:T(8,128)(2,1)} %cw.1) | copy-start | bytes 221188
  3.7 0.7 %copy-start.3 = (bf16[64,64]{1,0:T(8,128)(2,1)S(1)}, bf16[64,64]{1,0:T(8,128)(2,1)}, u32[]{:S(2)}) copy-start(bf16[64,64]{1,0:T(8,128)(2,1)} %pw.1) | copy-start | bytes 24580
  4.4 0.7 %copy-start.4 = (f32[64,7]{0,1:T(8,128)S(1)}, f32[64,7]{0,1:T(8,128)}, u32[]{:S(2)}) copy-start(f32[64,7]{0,1:T(8,128)} %param.6) | copy-start | bytes 5380

commit v3 on v2

v3 whole, which is shorter than its diff:
```python
import functools
import math

import jax
import jax.numpy as jnp
from jax import lax
from jax.experimental import pallas as pl
from jax.experimental.pallas import tpu as pltpu
from jax.sharding import PartitionSpec as P

F32, BF16 = jnp.float32, jnp.bfloat16
MESH = pl.DeviceIdType.MESH
TAPS = 7
RIM = 24
EDGE = 48
EDGE_G = 16
PLANE_UNITS = 32
EXTRA_UNITS = 9
FWD_UNROLL = 2
BWD_UNROLL = 4


def dot(a, b):
    return lax.dot_general(a, b, (((1,), (0,)), ((), ())), preferred_element_type=F32)


def dot_nt(a, b):
    return lax.dot_general(a, b, (((1,), (1,)), ((), ())), preferred_element_type=F32)


def select_matrix(rows, cols, offset=0):
    r = lax.broadcasted_iota(jnp.int32, (rows, cols), 0)
    c = lax.broadcasted_iota(jnp.int32, (rows, cols), 1)
    return jnp.where(c == r + offset, 1.0, 0.0).astype(BF16)


def loop(lo, hi, body):
    def step(i, carry):
        body(i)
        return carry

    lax.fori_loop(lo, hi, step, 0)


C0 = math.sqrt(2.0 / math.pi)
C1 = 0.044715 * C0


def gelu_cdf(pre):
    return 0.5 + 0.5 * jnp.tanh(pre * (C0 + C1 * (pre * pre)))


def gelu_slope(pre, cdf):
    return cdf + (pre * cdf) * (1.0 - cdf) * (2.0 * C0 + (6.0 * C1) * (pre * pre))


def kernel(
    low_chan, low_tm, n_chan, n_tm,
    sig_hbm, go_hbm, dw_hbm, pw_hbm, cw_hbm,
    feat, gsig, depth_out, point_out, conv_out,
    sig, go, dw, pw, cw, insem,
    send_l, send_r, halo_l, halo_r, row, corner_l, corner_r,
    xt, pre_s, cdf_s, ht, hp, go_ext, gt, gh_s, ga, gb, gd, acc_m, eye, wup, cwt, pw2, pwt2, wrow,
    part, plane_in, plane_x, mine, tower_in, tower_x, done,
    hssem, hrsem, ssem, rsem, xssem, xrsem,
):
    loads = [
        pltpu.make_async_copy(src, dst, insem.at[n])
        for n, (src, dst) in enumerate(
            ((sig_hbm, sig), (go_hbm, go), (dw_hbm, dw), (pw_hbm, pw), (cw_hbm, cw))
        )
    ]
    for load in loads:
        load.start()

    a, b = lax.axis_index("chan"), lax.axis_index("tm")
    plane = low_chan * low_tm
    hi_tm = n_tm // low_tm
    tower = (n_chan // low_chan) * hi_tm
    a_hi, b_hi = lax.div(a, low_chan), lax.div(b, low_tm)
    a_lo, b_lo = lax.rem(a, low_chan), lax.rem(b, low_tm)
    me = a_lo * low_tm + b_lo
    level = a_hi * hi_tm + b_hi
    before_a, after_a = a > 0, a < n_chan - 1
    before_b, after_b = b > 0, b < n_tm - 1
    both_of = jnp.logical_and

    rows_at = [lax.rem(a_lo + i, low_chan) for i in range(low_chan)]
    cols_at = [lax.rem(b_lo + j, low_tm) for j in range(low_tm)]
    in_plane = [
        (r * low_tm + c, (a_hi * low_chan + r, b_hi * low_tm + c))
        for i, r in enumerate(rows_at)
        for j, c in enumerate(cols_at)
        if i + j > 0
    ]
    hi_chan = n_chan // low_chan
    levels_a = [lax.rem(a_hi + i, hi_chan) * low_chan + a_lo for i in range(hi_chan)]
    levels_b = [lax.rem(b_hi + j, hi_tm) * low_tm + b_lo for j in range(hi_tm)]
    in_tower = [
        (ra, rb) for i, ra in enumerate(levels_a) for j, rb in enumerate(levels_b) if i + j > 0
    ]

    owners = [3 * u for u in range(EXTRA_UNITS)]
    own_x = both_of(lax.rem(me, 3) == 0, me < 3 * EXTRA_UNITS)
    unit_x = PLANE_UNITS + lax.rem(lax.div(me, 3), EXTRA_UNITS)

    around = [
        ((a, b - 1), before_b, after_b),
        ((a, b + 1), after_b, before_b),
        ((a + 1, b), after_a, before_a),
        ((a - 1, b), before_a, after_a),
        ((a + 1, b - 1), both_of(after_a, before_b), both_of(before_a, after_b)),
        ((a + 1, b + 1), both_of(after_a, after_b), both_of(before_a, before_b)),
        ((a - 1, b - 1), both_of(before_a, before_b), both_of(after_a, after_b)),
        ((a - 1, b + 1), both_of(before_a, after_b), both_of(after_a, before_b)),
    ]
    barrier = pltpu.get_barrier_semaphore()
    greeted = plane + tower - 2
    for device, there, _ in around:
        greeted = greeted + there.astype(jnp.int32)

        @pl.when(there)
        def _(device=device):
            pl.semaphore_signal(barrier, inc=1, device_id=device, device_id_type=MESH)

    for device in in_tower + [device for _, device in in_plane]:
        pl.semaphore_signal(barrier, inc=1, device_id=device, device_id_type=MESH)

    eye[...] = select_matrix(256, 256)
    for load in loads[2:]:
        load.wait()
    lane = lax.broadcasted_iota(jnp.int32, (64, 128), 1)
    sub = lax.broadcasted_iota(jnp.int32, (64, 128), 0)
    twice16 = jnp.where(lax.rem(lane, 64) == sub, 1.0, 0.0).astype(BF16)
    r128 = lax.broadcasted_iota(jnp.int32, (128, 128), 0)
    c128 = lax.broadcasted_iota(jnp.int32, (128, 128), 1)
    same = (r128 < 64) == (c128 < 64)
    wide = dot(pw[...], twice16)
    pw2[...] = jnp.where(same, jnp.concatenate([wide, wide], axis=0), 0.0).astype(BF16)
    eye64 = select_matrix(64, 64)
    turned = dot(dot_nt(eye64, pw[...]).astype(BF16), twice16)
    pwt2[...] = jnp.where(same, jnp.concatenate([turned, turned], axis=0), 0.0).astype(BF16)
    zero64 = jnp.zeros((64, 64), BF16)
    wup[128:256, 0:128] = jnp.zeros((128, 128), BF16)
    for j in range(3):
        first = dot_nt(eye64, jnp.concatenate([zero64, cw[0, j]], axis=0)).astype(BF16)
        rest = dot_nt(eye64, jnp.concatenate([cw[1, j], cw[2, j]], axis=0)).astype(BF16)
        cwt[:, j * 256 : j * 256 + 128] = first
        cwt[:, j * 256 + 128 : j * 256 + 256] = rest
        at = {1: (0, 0), 2: (0, 128), 0: (128, 128)}[j]
        wup[at[0] : at[0] + 64, at[1] : at[1] + 128] = rest
        wup[at[0] + 64 : at[0] + 128, at[1] : at[1] + 128] = first
    wrow[0:TAPS, 0:64] = dw[...]
    wrow[0:TAPS, 64:128] = dw[...]
    wrow[TAPS:, :] = jnp.zeros((1, 128), F32)

    loads[1].wait()
    loads[0].wait()

    pick_s, pick_g = select_matrix(EDGE, 128), select_matrix(EDGE_G, 128)
    pick_sr, pick_gr = select_matrix(EDGE, 128, 128 - EDGE), select_matrix(EDGE_G, 128, 128 - EDGE_G)
    zero16 = jnp.zeros((64, 128), BF16)
    for m in range(-1, 8):
        for pick, pick2, lanes, glanes, dst in (
            (pick_s, pick_g, slice(0, 128), slice(0, 128), send_l),
            (pick_sr, pick_gr, slice(384, 512), slice(128, 256), send_r),
        ):
            if m >= 0:
                dst[m + 1, 0:EDGE] = dot_nt(pick, sig[m, :, lanes]).astype(BF16)
            low = go[m, :, glanes] if m >= 0 else zero16
            high = go[m + 1, :, glanes] if m < 7 else zero16
            dst[m + 1, EDGE:] = dot_nt(pick2, jnp.concatenate([low, high], axis=0)).astype(BF16)

    pl.semaphore_wait(barrier, greeted)
    pieces = [
        (send_l.at[pl.ds(1, 8)], halo_r.at[pl.ds(1, 8)]),
        (send_r.at[pl.ds(1, 8)], halo_l.at[pl.ds(1, 8)]),
        (sig.at[7, pl.ds(64, 64)], row),
        (go.at[0], go_ext.at[pl.ds(512, 64)]),
        (send_l.at[8, pl.ds(0, EDGE)], halo_r.at[0, pl.ds(0, EDGE)]),
        (send_r.at[8, pl.ds(0, EDGE)], halo_l.at[0, pl.ds(0, EDGE)]),
        (send_l.at[0, pl.ds(EDGE, EDGE_G)], corner_r),
        (send_r.at[0, pl.ds(EDGE, EDGE_G)], corner_l),
    ]
    copies = [
        pltpu.make_async_remote_copy(
            src_ref=src, dst_ref=dst, send_sem=hssem.at[n], recv_sem=hrsem.at[n],
            device_id=around[n][0], device_id_type=MESH,
        )
        for n, (src, dst) in enumerate(pieces)
    ]
    for n in (2, 3, 0, 1, 4, 5, 6, 7):

        @pl.when(around[n][1])
        def _(n=n):
            copies[n].start()

    def arrive(n):
        dst = pieces[n][1]

        @pl.when(around[n][2])
        def _():
            copies[n].wait_recv()

        @pl.when(jnp.logical_not(around[n][2]))
        def _():
            dst[...] = jnp.zeros(dst.shape, BF16)

    def turn(n, x):
        unit = eye[...]
        xt[n, 48:304] = dot_nt(unit, x[:, 0:256])
        xt[n, 304:560] = dot_nt(unit, x[:, 256:512])

    for m in range(8):
        turn(m + 1, sig[m])
    go_ext[0:512] = go[...].reshape(512, 256)

    def taps(n, lo, count):
        low = wrow[0:1, :] * xt[n, lo : lo + count]
        for k in range(1, TAPS):
            low = low + wrow[k : k + 1, :] * xt[n, lo + 8 * k : lo + 8 * k + count]
        return low.astype(BF16)

    def forward(n, lo, count, keep=True):
        pre = dot(taps(n, lo, count), pw2[...])
        cdf = gelu_cdf(pre)
        ht[n, lo : lo + count] = xt[n, lo + 24 : lo + 24 + count] + pre * cdf
        if keep:
            pre_s[n, lo : lo + count] = pre
            cdf_s[n, lo : lo + count] = cdf

    def forward_some(i):
        for s in range(FWD_UNROLL):
            forward(FWD_UNROLL * i + 1 + s, 48, 464)

    loop(0, 8 // FWD_UNROLL, forward_some)
    arrive(0)
    arrive(1)
    for lo, src, at in ((0, halo_l, 0), (512, halo_r, 560)):
        for n in range(1, 9):
            xt[n, at : at + EDGE] = src[n, 0:EDGE].astype(F32)
        pre = dot(jnp.concatenate([taps(n, lo, 48) for n in range(1, 9)], axis=0), pw2[...])
        cdf = gelu_cdf(pre)
        value = pre * cdf
        for n in range(1, 9):
            own_rows = slice((n - 1) * 48, n * 48)
            ht[n, lo : lo + 48] = xt[n, lo + 24 : lo + 72] + value[own_rows]
            pre_s[n, lo : lo + 48] = pre[own_rows]
            cdf_s[n, lo : lo + 48] = cdf[own_rows]
    arrive(2)
    arrive(4)
    arrive(5)
    xt[0, 0:EDGE] = halo_l[0, 0:EDGE].astype(F32)
    turn(0, jnp.concatenate([jnp.zeros((64, 512), BF16), row[...]], axis=0))
    xt[0, 560:608] = halo_r[0, 0:EDGE].astype(F32)
    forward(0, 16, 528, False)

    @pl.when(b == 0)
    def _():
        for n in range(9):
            ht[n, 23:24] = jnp.zeros((1, 128), F32)
            pre_s[n, 0:24] = jnp.zeros((24, 128), F32)
            cdf_s[n, 0:24] = jnp.zeros((24, 128), F32)

    @pl.when(b == n_tm - 1)
    def _():
        for n in range(9):
            pre_s[n, 536:560] = jnp.zeros((24, 128), F32)
            cdf_s[n, 536:560] = jnp.zeros((24, 128), F32)

    for n in range(9):
        for j in range(3):
            hp[j, n] = ht[n, pl.ds(23 + j, 256, stride=2), :].astype(BF16)

    grads = []
    for j in range(3):
        total = jnp.zeros((64, 256), F32)
        for o in range(8):
            total = total + dot(go[o], jnp.concatenate([hp[j, o], hp[j, o + 1]], axis=1))
        grads.append(total)
        put(part, 8 * j, total[:, 128:256])
    put(part, 24, jnp.where(lane < 64, pltpu.roll(grads[0][:, 0:128], 64, 1), grads[1][:, 0:128]))
    last = grads[2][:, 0:128]

    def remote(src, dst, s, r, device):
        return pltpu.make_async_remote_copy(
            src_ref=src, dst_ref=dst, send_sem=s, recv_sem=r, device_id=device, device_id_type=MESH
        )

    def several(ref, count, sem_s, sem_r):
        at = ref.at[pl.ds(0, count)]
        return remote(at, at, sem_s, sem_r, in_plane[0][1])

    for p, device in in_plane:
        remote(part.at[p], plane_in.at[me], ssem.at[0], rsem.at[0], device).start()

    arrive(3)
    arrive(6)
    arrive(7)
    for halo, corner in ((halo_l, corner_l), (halo_r, corner_r)):
        halo[8, EDGE:] = (halo[8, EDGE:].astype(F32) + corner[...].astype(F32)).astype(BF16)

    def backward(i):
        unit = eye[...]
        lhs, rhs = [], []
        for s in range(BWD_UNROLL):
            m = BWD_UNROLL * i + s
            x = go_ext[pl.ds(pl.multiple_of(m * 64, 64), 128), :]
            gt[s, 0:16] = halo_l[m + 1, EDGE:].astype(F32)
            gt[s, 16:272] = dot_nt(unit, x)
            gt[s, 272:288] = halo_r[m + 1, EDGE:].astype(F32)
            gt[s, 288:296] = jnp.zeros((8, 128), F32)
            both = jnp.concatenate([gt[s, 0:288].astype(BF16), gt[s, 1:289].astype(BF16)], axis=1)
            up = dot(both, wup[...])
            gh_s[m, pl.ds(0, 288, stride=2), :] = up[:, 0:128]
            gh_s[m, pl.ds(1, 288, stride=2), :] = up[:, 128:256]
            mixed = gh_s[m, 8:568] * gelu_slope(pre_s[m + 1], cdf_s[m + 1])
            ga[m] = mixed.astype(BF16)
            gb[s, 0:552] = mixed[8:560].astype(BF16)
            shifted = []
            for k in range(TAPS):
                at = 48 - 8 * k
                shifted.append(ga[m, at : at + 512] if k % 2 == 0 else gb[s, at - 8 : at + 504])
            lhs.append(sig[m])
            rhs.append(jnp.concatenate(shifted, axis=1))
        acc_m[...] += dot(jnp.concatenate(lhs, axis=1), jnp.concatenate(rhs, axis=0))

    acc_m[...] = jnp.zeros_like(acc_m)
    dw_col = jnp.transpose(jnp.concatenate([wrow[...], jnp.zeros((120, 128), F32)], axis=0))
    loop(0, 8 // BWD_UNROLL, backward)

    point = jnp.zeros((64, 128), F32)
    pw_wide = jnp.where(lane < 64, dot(pw[...], twice16), 0.0)
    products = []
    for k in range(TAPS):
        tap = acc_m[0:64, k * 128 : k * 128 + 128] + pltpu.roll(
            acc_m[64:128, k * 128 : k * 128 + 128], 64, 1
        )
        point = point + dw_col[0:64, k : k + 1] * tap
        products.append(tap * pw_wide)
    put(part, 32, jnp.where(lane < 64, point, last))
    product = jnp.concatenate(products, axis=1)
    piece_h = product.astype(BF16)
    rest = product - piece_h.astype(F32)
    piece_m = rest.astype(BF16)
    piece_l = (rest - piece_m.astype(F32)).astype(BF16)
    tap_of = lax.broadcasted_iota(jnp.int32, (8, TAPS * 128), 1)
    row_of = lax.broadcasted_iota(jnp.int32, (8, TAPS * 128), 0)
    ones = jnp.where(lax.div(tap_of, 128) == row_of, 1.0, 0.0).astype(BF16)
    depth = dot_nt(ones, piece_h) + (dot_nt(ones, piece_m) + dot_nt(ones, piece_l))
    part[40] = jnp.concatenate([depth, jnp.zeros((8, 64), F32)], axis=1)

    for u, p in enumerate(owners):

        @pl.when(me != p)
        def _(u=u, p=p):
            device = (a_hi * low_chan + p // low_tm, b_hi * low_tm + p % low_tm)
            remote(part.at[PLANE_UNITS + u], plane_x.at[me], xssem.at[0], xrsem.at[0], device).start()

    for o in range(8):
        wide_taps = jnp.concatenate([hp[j, o + s] for j in range(3) for s in range(2)], axis=1)
        feat[o] = dot_nt(cwt[...], wide_taps).astype(BF16)

    plane_in[me] = part[me]
    several(plane_in, plane - 1, ssem.at[0], rsem.at[0]).wait_recv()
    total = plane_in[0]
    for d in range(1, plane):
        total = total + plane_in[d]
    mine[0] = total
    for device in in_tower:
        remote(mine.at[0], tower_in.at[level], ssem.at[1], rsem.at[1], device).start()

    def finish(m):
        unit = eye[0:128, 0:128]
        s = m % 4
        gd[s] = dot(ga[m], pwt2[...])
        total = gh_s[m, 32:544]
        for k in range(TAPS):
            at = 48 - 8 * k
            total = total + wrow[k : k + 1, :] * gd[s, at : at + 512]
        gsig[m] = dot_nt(unit, total.astype(BF16)).astype(BF16)

    for m in range(4):
        finish(m)

    @pl.when(own_x)
    def _():
        plane_x[me] = part[unit_x]
        several(plane_x, plane - 1, xssem.at[0], xrsem.at[0]).wait_recv()
        total = plane_x[0]
        for d in range(1, plane):
            total = total + plane_x[d]
        mine[1] = total
        for device in in_tower:
            remote(mine.at[1], tower_x.at[level], xssem.at[1], xrsem.at[1], device).start()

    tower_in[level] = mine[0]
    several(tower_in, tower - 1, ssem.at[1], rsem.at[1]).wait_recv()
    total = tower_in[0]
    for q in range(1, tower):
        total = total + tower_in[q]
    done[me] = total
    for _, device in in_plane:
        remote(done.at[me], done.at[me], ssem.at[2], rsem.at[2], device).start()

    for m in range(4, 8):
        finish(m)

    @pl.when(own_x)
    def _():
        tower_x[level] = mine[1]
        several(tower_x, tower - 1, xssem.at[1], xrsem.at[1]).wait_recv()
        total = tower_x[0]
        for q in range(1, tower):
            total = total + tower_x[q]
        done[unit_x] = total
        for _, device in in_plane:
            remote(done.at[unit_x], done.at[unit_x], xssem.at[2], xrsem.at[2], device).start()

    def tile(n):
        return done[n * 8 : n * 8 + 8].reshape(64, 128)

    def conv_tile(n):
        zero = jnp.zeros((64, 128), F32)
        return jnp.transpose(jnp.concatenate([tile(n), zero], axis=0))

    several(plane_in, plane - 1, ssem.at[2], rsem.at[2]).wait_recv()
    for n in range(4):
        turned = conv_tile(n)
        for half in range(2):
            i, j = (half + 1, n) if n < 3 else (0, half)
            conv_out[i, j] = turned[half * 64 : half * 64 + 64, 0:64]

    @pl.when(own_x)
    def _():
        several(plane_in, EXTRA_UNITS - 1, xssem.at[2], xrsem.at[2]).wait_recv()

    @pl.when(jnp.logical_not(own_x))
    def _():
        several(plane_in, EXTRA_UNITS, xssem.at[2], xrsem.at[2]).wait_recv()

    conv_out[0, 2] = conv_tile(4)[64:128, 0:64]
    point_out[...] = tile(4)[:, 0:64]
    depth_out[...] = done[40][0:TAPS, 0:64]

    for n in range(8):

        @pl.when(around[n][1])
        def _(n=n):
            copies[n].wait_send()

    several(plane_in, plane - 1, ssem.at[0], rsem.at[0]).wait_send()
    several(tower_in, tower - 1, ssem.at[1], rsem.at[1]).wait_send()
    several(plane_in, plane - 1, ssem.at[2], rsem.at[2]).wait_send()

    @pl.when(own_x)
    def _():
        several(plane_in, EXTRA_UNITS - 1, xssem.at[0], xrsem.at[0]).wait_send()
        several(tower_in, tower - 1, xssem.at[1], xrsem.at[1]).wait_send()
        several(plane_in, plane - 1, xssem.at[2], xrsem.at[2]).wait_send()

    @pl.when(jnp.logical_not(own_x))
    def _():
        several(plane_in, EXTRA_UNITS, xssem.at[0], xrsem.at[0]).wait_send()


def emit_kernel(*refs):
    srcs, dsts, sem = refs[:5], refs[5:10], refs[10]
    copies = [pltpu.make_async_copy(src, dst, sem.at[n]) for n, (src, dst) in enumerate(zip(srcs, dsts))]
    for copy in copies:
        copy.start()
    for copy in copies:
        copy.wait()


def put(ref, unit, tile):
    ref[unit : unit + 8] = tile.reshape(8, 8, 128)


def solution(mesh):
    n_chan, n_tm = mesh.shape["chan"], mesh.shape["tm"]
    low_chan, low_tm = 8, 4
    plane = low_chan * low_tm
    tower = n_chan * n_tm // plane
    whole = pl.BlockSpec(memory_space=pltpu.VMEM)
    sems = pltpu.SemaphoreType.DMA((3,))
    hbm = pl.BlockSpec(memory_space=pltpu.MemorySpace.HBM)
    vm = pltpu.VMEM

    def local(signal, depth_weight, point_weight, conv_weight, grad_out):
        outs = pl.pallas_call(
            functools.partial(kernel, low_chan, low_tm, n_chan, n_tm),
            out_shape=(shapes := [
                jax.ShapeDtypeStruct((8, 64, 256), BF16),
                jax.ShapeDtypeStruct((8, 128, 512), BF16),
                jax.ShapeDtypeStruct((TAPS, 64), F32),
                jax.ShapeDtypeStruct((64, 64), F32),
                jax.ShapeDtypeStruct((3, 3, 64, 64), F32),
            ]),
            in_specs=[hbm] * 5,
            out_specs=[whole] * 5,
            scratch_shapes=[
                vm((8, 128, 512), BF16),
                vm((8, 64, 256), BF16),
                vm((TAPS, 64), F32),
                vm((64, 64), BF16),
                vm((3, 3, 64, 64), BF16),
                pltpu.SemaphoreType.DMA((5,)),
                vm((9, 64, 128), BF16),
                vm((9, 64, 128), BF16),
                vm((9, 64, 128), BF16),
                vm((9, 64, 128), BF16),
                vm((64, 512), BF16),
                vm((EDGE_G, 128), BF16),
                vm((EDGE_G, 128), BF16),
                vm((9, 608, 128), F32),
                vm((9, 560, 128), F32),
                vm((9, 560, 128), F32),
                vm((9, 560, 128), F32),
                vm((3, 9, 256, 128), BF16),
                vm((576, 256), BF16),
                vm((BWD_UNROLL, 296, 128), F32),
                vm((8, 576, 128), F32),
                vm((8, 560, 128), BF16),
                vm((BWD_UNROLL, 560, 128), BF16),
                vm((4, 560, 128), F32),
                vm((128, 896), F32),
                vm((256, 256), BF16),
                vm((256, 256), BF16),
                vm((64, 768), BF16),
                vm((128, 128), BF16),
                vm((128, 128), BF16),
                vm((8, 128), F32),
                vm((PLANE_UNITS + EXTRA_UNITS, 8, 128), F32),
                vm((plane, 8, 128), F32),
                vm((plane, 8, 128), F32),
                vm((2, 8, 128), F32),
                vm((tower, 8, 128), F32),
                vm((tower, 8, 128), F32),
                vm((PLANE_UNITS + EXTRA_UNITS, 8, 128), F32),
                pltpu.SemaphoreType.DMA((8,)),
                pltpu.SemaphoreType.DMA((8,)),
                sems, sems, sems, sems,
            ],
            compiler_params=pltpu.CompilerParams(
                collective_id=0, has_side_effects=True, vmem_limit_bytes=48 * 1024 * 1024
            ),
            name="step",
        )(
            *(
                pltpu.with_memory_space_constraint(x, pltpu.MemorySpace.HBM)
                for x in (signal.reshape(8, 128, 512), grad_out, depth_weight.T, point_weight, conv_weight)
            )
        )
        feat, gsig, depth, point, conv = pl.pallas_call(
            emit_kernel,
            out_shape=shapes,
            in_specs=[pl.BlockSpec(memory_space=pl.ANY)] * 5,
            out_specs=[pl.BlockSpec(memory_space=pl.ANY)] * 5,
            scratch_shapes=[pltpu.SemaphoreType.DMA((5,))],
            compiler_params=pltpu.CompilerParams(vmem_limit_bytes=1024 * 1024),
            name="emit",
        )(*outs)
        return feat, gsig.reshape(16, 64, 512), depth.T, point, conv

    in_specs = (P("chan", None, "tm"), P(), P(), P(), P("chan", None, "tm"))
    out_specs = (P("chan", None, "tm"), P("chan", None, "tm"), P(), P(), P())
    return jax.shard_map(local, mesh=mesh, in_specs=in_specs, out_specs=out_specs, check_vma=False)
```

time: 53.1 us -> 41.2 us (0.78)
  local copies, waits for them, and re-layouts: 8.07 us -> 0 us
  Pallas kernels: 44.1 us -> 40.5 us
    unnamed x15 -> x0, local copies, waits for them, and re-layouts: 8.07 us -> none
    pallas_call x1, Pallas kernels: 44.1 us -> 39.3 us  [local(): pl.pallas_call(functools.partial(kernel, low_chan, low_tm, n_chan, n_tm),...]
    pallas_call x0 -> x1, Pallas kernels: none -> 1.21 us  [local(): pl.pallas_call(emit_kernel, out_shape=shapes, in_specs=[pl.BlockSpec(memo...]
where the time goes in v3:
time: 41.2 us; the launch traced here: 41.1 us
  Pallas kernels  40.5 us (98%)
  between operations  0.64 us (2%)
    pallas_call x1, Pallas kernels, local(): pl.pallas_call(functools.partial(kernel, low_chan, low_tm, n_chan, n_tm),...  39.3 us
    pallas_call x1, Pallas kernels, local(): pl.pallas_call(emit_kernel, out_shape=shapes, in_specs=[pl.BlockSpec(memo...  1.21 us

profile of v3, /device:TPU:1, one launch (start us, length us, event | category | flops | bytes accessed | tf_op | source)
XLA Modules:
  0.0 41.1 jit_solution(11236795131506754745)
XLA Ops:
  0.6 39.3 %step.1 = (bf16[8,64,256]{2,1,0:T(8,128)(2,1)S(1)}, bf16[8,128,512]{2,1,0:T(8,128)(2,1)S(1)}, f32[7,64]{1,0:T(8,128)S(1)}, f32[64,64]{1,0:T(8,128)S(1)}, f32[3,3,64,64]{3,2,1,0:T(8,128)S(1)}) custom-call(bf16[8,128,512]{2,1,0:T(8,128)(2,1)} %bitcast.4, bf16[8,64,256]{2,1,0:T(8,128)(2,1)} %go_hbm.1, f32[7,64]{1,0:T(8,128)} %bitcast.5, bf16[64,64]{1,0:T(8,128)(2,1)} %pw_hbm.1, ...), custom_call_target="tpu_custom_call" | custom-call | tf_op jit(solution)/shard_map/step/pallas_call | solution.py:491
  39.9 1.2 %emit.1 = (bf16[8,64,256]{2,1,0:T(8,128)(2,1)}, bf16[8,128,512]{2,1,0:T(8,128)(2,1)}, f32[7,64]{1,0:T(8,128)}, f32[64,64]{1,0:T(8,128)}, f32[3,3,64,64]{3,2,1,0:T(8,128)}) custom-call(bf16[8,64,256]{2,1,0:T(8,128)(2,1)S(1)} %get-tuple-element.15.refs_0_, bf16[8,128,512]{2,1,0:T(8,128)(2,1)S(1)} %get-tuple-element.16.refs_1_, ...), custom_call_target="tpu_custom_call" | custom-call | tf_op jit(solution)/shard_map/emit/pallas_call | solution.py:555

commit v4 on v3

--- a/solution.py
+++ b/solution.py
@@ -16,7 +16,6 @@
 EDGE_G = 16
 PLANE_UNITS = 32
 EXTRA_UNITS = 9
-FWD_UNROLL = 2
 BWD_UNROLL = 4
 
 
@@ -60,7 +59,7 @@
     feat, gsig, depth_out, point_out, conv_out,
     sig, go, dw, pw, cw, insem,
     send_l, send_r, halo_l, halo_r, row, corner_l, corner_r,
-    xt, pre_s, cdf_s, ht, hp, go_ext, gt, gh_s, ga, gb, gd, acc_m, eye, wup, cwt, pw2, pwt2, wrow,
+    xt, pre_s, cdf_s, ht, hp, go_next, gt, gh_s, ga, gb, gd, acc_m, eye, wup, cwt, pw2, pwt2, wrow,
     part, plane_in, plane_x, mine, tower_in, tower_x, done,
     hssem, hrsem, ssem, rsem, xssem, xrsem,
 ):
@@ -176,7 +175,7 @@
         (send_l.at[pl.ds(1, 8)], halo_r.at[pl.ds(1, 8)]),
         (send_r.at[pl.ds(1, 8)], halo_l.at[pl.ds(1, 8)]),
         (sig.at[7, pl.ds(64, 64)], row),
-        (go.at[0], go_ext.at[pl.ds(512, 64)]),
+        (go.at[0], go_next),
         (send_l.at[8, pl.ds(0, EDGE)], halo_r.at[0, pl.ds(0, EDGE)]),
         (send_r.at[8, pl.ds(0, EDGE)], halo_l.at[0, pl.ds(0, EDGE)]),
         (send_l.at[0, pl.ds(EDGE, EDGE_G)], corner_r),
@@ -211,9 +210,6 @@
         xt[n, 48:304] = dot_nt(unit, x[:, 0:256])
         xt[n, 304:560] = dot_nt(unit, x[:, 256:512])
 
-    for m in range(8):
-        turn(m + 1, sig[m])
-    go_ext[0:512] = go[...].reshape(512, 256)
 
     def taps(n, lo, count):
         low = wrow[0:1, :] * xt[n, lo : lo + count]
@@ -229,11 +225,27 @@
             pre_s[n, lo : lo + count] = pre
             cdf_s[n, lo : lo + count] = cdf
 
-    def forward_some(i):
-        for s in range(FWD_UNROLL):
-            forward(FWD_UNROLL * i + 1 + s, 48, 464)
-
-    loop(0, 8 // FWD_UNROLL, forward_some)
+    def widen(m, lo, count):
+        here, later = gt[m, lo : lo + count], gt[m, lo + 1 : lo + count + 1]
+        return jnp.concatenate([here.astype(BF16), later.astype(BF16)], axis=1)
+
+    def interleave(m, at, up):
+        count = up.shape[0]
+        gh_s[m, pl.ds(at, count, stride=2), :] = up[:, 0:128]
+        gh_s[m, pl.ds(at + 1, count, stride=2), :] = up[:, 128:256]
+
+    def split(n, lo, count):
+        for j in range(3):
+            hp[j, n, lo : lo + count] = ht[n, pl.ds(23 + j + 2 * lo, count, stride=2), :].astype(BF16)
+
+    for m in range(8):
+        turn(m + 1, sig[m])
+        forward(m + 1, 48, 464)
+        if m < 7:
+            gt[m, 16:272] = dot_nt(eye[...], jnp.concatenate([go[m], go[m + 1]], axis=0))
+            interleave(m, 32, dot(widen(m, 16, 240), wup[...]))
+        split(m + 1, 16, 224)
+
     arrive(0)
     arrive(1)
     for lo, src, at in ((0, halo_l, 0), (512, halo_r, 560)):
@@ -268,9 +280,10 @@
             pre_s[n, 536:560] = jnp.zeros((24, 128), F32)
             cdf_s[n, 536:560] = jnp.zeros((24, 128), F32)
 
-    for n in range(9):
-        for j in range(3):
-            hp[j, n] = ht[n, pl.ds(23 + j, 256, stride=2), :].astype(BF16)
+    split(0, 0, 256)
+    for n in range(1, 9):
+        split(n, 0, 16)
+        split(n, 240, 16)
 
     grads = []
     for j in range(3):
@@ -300,20 +313,22 @@
     for halo, corner in ((halo_l, corner_l), (halo_r, corner_r)):
         halo[8, EDGE:] = (halo[8, EDGE:].astype(F32) + corner[...].astype(F32)).astype(BF16)
 
+    for m in range(8):
+        gt[m, 0:16] = halo_l[m + 1, EDGE:].astype(F32)
+        gt[m, 272:288] = halo_r[m + 1, EDGE:].astype(F32)
+        gt[m, 288:296] = jnp.zeros((8, 128), F32)
+    gt[7, 16:272] = dot_nt(eye[...], jnp.concatenate([go[7], go_next[...]], axis=0))
+    rims = [widen(m, lo, count) for m in range(7) for lo, count in ((0, 16), (256, 32))]
+    up = dot(jnp.concatenate(rims + [widen(7, 0, 288)], axis=0), wup[...])
+    for m in range(7):
+        interleave(m, 0, up[48 * m : 48 * m + 16])
+        interleave(m, 512, up[48 * m + 16 : 48 * m + 48])
+    interleave(7, 0, up[336:624])
+
     def backward(i):
-        unit = eye[...]
         lhs, rhs = [], []
         for s in range(BWD_UNROLL):
             m = BWD_UNROLL * i + s
-            x = go_ext[pl.ds(pl.multiple_of(m * 64, 64), 128), :]
-            gt[s, 0:16] = halo_l[m + 1, EDGE:].astype(F32)
-            gt[s, 16:272] = dot_nt(unit, x)
-            gt[s, 272:288] = halo_r[m + 1, EDGE:].astype(F32)
-            gt[s, 288:296] = jnp.zeros((8, 128), F32)
-            both = jnp.concatenate([gt[s, 0:288].astype(BF16), gt[s, 1:289].astype(BF16)], axis=1)
-            up = dot(both, wup[...])
-            gh_s[m, pl.ds(0, 288, stride=2), :] = up[:, 0:128]
-            gh_s[m, pl.ds(1, 288, stride=2), :] = up[:, 128:256]
             mixed = gh_s[m, 8:568] * gelu_slope(pre_s[m + 1], cdf_s[m + 1])
             ga[m] = mixed.astype(BF16)
             gb[s, 0:552] = mixed[8:560].astype(BF16)
@@ -357,10 +372,6 @@
             device = (a_hi * low_chan + p // low_tm, b_hi * low_tm + p % low_tm)
             remote(part.at[PLANE_UNITS + u], plane_x.at[me], xssem.at[0], xrsem.at[0], device).start()
 
-    for o in range(8):
-        wide_taps = jnp.concatenate([hp[j, o + s] for j in range(3) for s in range(2)], axis=1)
-        feat[o] = dot_nt(cwt[...], wide_taps).astype(BF16)
-
     plane_in[me] = part[me]
     several(plane_in, plane - 1, ssem.at[0], rsem.at[0]).wait_recv()
     total = plane_in[0]
@@ -369,6 +380,10 @@
     mine[0] = total
     for device in in_tower:
         remote(mine.at[0], tower_in.at[level], ssem.at[1], rsem.at[1], device).start()
+
+    for o in range(8):
+        wide_taps = jnp.concatenate([hp[j, o + s] for j in range(3) for s in range(2)], axis=1)
+        feat[o] = dot_nt(cwt[...], wide_taps).astype(BF16)
 
     def finish(m):
         unit = eye[0:128, 0:128]
@@ -518,8 +533,8 @@
                 vm((9, 560, 128), F32),
                 vm((9, 560, 128), F32),
                 vm((3, 9, 256, 128), BF16),
-                vm((576, 256), BF16),
-                vm((BWD_UNROLL, 296, 128), F32),
+                vm((64, 256), BF16),
+                vm((8, 296, 128), F32),
                 vm((8, 576, 128), F32),
                 vm((8, 560, 128), BF16),
                 vm((BWD_UNROLL, 560, 128), BF16),

time: 41.2 us -> 40.6 us (0.985)
  Pallas kernels: 40.5 us -> 39.8 us
    pallas_call x1, Pallas kernels: 39.3 us -> 38.6 us  [local(): pl.pallas_call(functools.partial(kernel, low_chan, low_tm, n_chan, n_tm),...]
where the time goes in v4:
time: 40.6 us; the launch traced here: 40.4 us
  Pallas kernels  39.8 us (98%)
  between operations  0.64 us (2%)
    pallas_call x1, Pallas kernels, local(): pl.pallas_call(functools.partial(kernel, low_chan, low_tm, n_chan, n_tm),...  38.6 us
    pallas_call x1, Pallas kernels, local(): pl.pallas_call(emit_kernel, out_shape=shapes, in_specs=[pl.BlockSpec(memo...  1.21 us

profile of v4, /device:TPU:1, one launch (start us, length us, event | category | flops | bytes accessed | tf_op | source)
XLA Modules:
  0.0 40.4 jit_solution(9509133637005042207)
XLA Ops:
  0.6 38.6 %step.1 = (bf16[8,64,256]{2,1,0:T(8,128)(2,1)S(1)}, bf16[8,128,512]{2,1,0:T(8,128)(2,1)S(1)}, f32[7,64]{1,0:T(8,128)S(1)}, f32[64,64]{1,0:T(8,128)S(1)}, f32[3,3,64,64]{3,2,1,0:T(8,128)S(1)}) custom-call(bf16[8,128,512]{2,1,0:T(8,128)(2,1)} %bitcast.4, bf16[8,64,256]{2,1,0:T(8,128)(2,1)} %go_hbm.1, f32[7,64]{1,0:T(8,128)} %bitcast.5, bf16[64,64]{1,0:T(8,128)(2,1)} %pw_hbm.1, ...), custom_call_target="tpu_custom_call" | custom-call | tf_op jit(solution)/shard_map/step/pallas_call | solution.py:506
  39.2 1.2 %emit.1 = (bf16[8,64,256]{2,1,0:T(8,128)(2,1)}, bf16[8,128,512]{2,1,0:T(8,128)(2,1)}, f32[7,64]{1,0:T(8,128)}, f32[64,64]{1,0:T(8,128)}, f32[3,3,64,64]{3,2,1,0:T(8,128)}) custom-call(bf16[8,64,256]{2,1,0:T(8,128)(2,1)S(1)} %get-tuple-element.15.refs_0_, bf16[8,128,512]{2,1,0:T(8,128)(2,1)S(1)} %get-tuple-element.16.refs_1_, ...), custom_call_target="tpu_custom_call" | custom-call | tf_op jit(solution)/shard_map/emit/pallas_call | solution.py:570
